TPU v7x, 32 devices: a whole 2x2x4 slice. The times are simulated.
32 devices in a mesh: fsdp: 16 (over z, y, x), tp: 2 (over core).
Axes of the slice: x: 2, y: 2, z: 4, core: 2. Of those that a mesh axis runs over, the one named last changes fastest.
Arguments:
- owner: int32 [2, 7], replicated, may hold values from 0 to 15, as said below
- grads: bfloat16 [2, 896, 2, 8320], P(None, 'fsdp', 'tp')
- weights: float32 [2, 896, 2, 8320], P(None, 'fsdp', 'tp'), may hold values from -0.1875 to 0.1875
- adam_m: float32 [2, 896, 2, 8320], P(None, 'fsdp', 'tp'), may hold values from -0.4375 to 0.4375
- adam_v: float32 [2, 896, 2, 8320], P(None, 'fsdp', 'tp'), may hold values from 0.0001 to 0.1
- stats: float32 [16, 896, 896], P('fsdp', 'tp')
- roots: bfloat16 [16, 896, 896], P('fsdp', 'tp')
- vec_weight: float32 [2, 2944], P(None, ('fsdp', 'tp')), may hold values from 0.5 to 1.5
- vec_grad: bfloat16 [2, 2944], P(None, ('fsdp', 'tp')), may hold values from -1.5 to 1.5
- vec_m: float32 [2, 2944], P(None, ('fsdp', 'tp')), may hold values from -0.4375 to 0.4375
- vec_v: float32 [2, 2944], P(None, ('fsdp', 'tp')), may hold values from 0.0001 to 0.1
Outputs:
- weights_new: float32 [2, 896, 2, 8320], P(None, 'fsdp', 'tp')
- adam_m_new: float32 [2, 896, 2, 8320], P(None, 'fsdp', 'tp')
- adam_v_new: float32 [2, 896, 2, 8320], P(None, 'fsdp', 'tp')
- stats_new: float32 [16, 896, 896], P('fsdp', 'tp')
- vec_weight_new: float32 [2, 2944], P(None, ('fsdp', 'tp'))
- vec_m_new: float32 [2, 2944], P(None, ('fsdp', 'tp'))
- vec_v_new: float32 [2, 2944], P(None, ('fsdp', 'tp'))
Inputs may be any that keep to these rules, and one draw needn't show every extreme that they name: owner[l, t] is the index along fsdp of the chip whose slot holds the statistic of kind t of layer l; all 14 values are distinct, so a chip owns at most one matrix and some chips own none.
All inputs are finite; a program needn't handle non-finite values.
Results may differ from a plain program's by a relative error of at most 0.0015.
Values may be sent and summed in bfloat16 or wider, within the bound.
No kernel may reach another device: no remote copies, remote signals or barrier semaphores. Data moves between devices by JAX's collectives and lax.ppermute only.
A program may use at most 192 MiB of HBM per device.

v0:
```python
import jax
import jax.numpy as jnp
from jax import lax
from jax.sharding import PartitionSpec as P

FF = 4864
QW = 896
KW = 128


def half_widths():
    return [QW // 2, KW // 2, KW // 2, QW // 2, FF // 2, FF // 2, FF // 2]


def column_starts(widths):
    starts = []
    position = 0
    for wide in widths:
        starts.append(position)
        position = position + wide
    return starts


def kind_sums(values, widths, starts):
    return jnp.stack(
        [
            jnp.sum(values[:, :, starts[kind] : starts[kind] + widths[kind]], axis=(1, 2))
            for kind in range(7)
        ],
        axis=1,
    )


def gram_rows(left, right):
    return lax.dot_general(
        left, right, (((1,), (1,)), ((), ())), preferred_element_type=jnp.float32
    )


def on_device(
    owner, grads, weights, adam_m, adam_v, stats, roots, vec_weight, vec_grad, vec_m, vec_v
):
    widths = half_widths()
    starts = column_starts(widths)
    classes = [widths[0], widths[1], widths[4]]
    class_table = jnp.array([0, 1, 1, 0, 2, 2, 2], jnp.int32)
    chips = lax.axis_size("fsdp")
    layers = grads.shape[0]
    rows = grads.shape[1]
    capacity = FF // 2
    model_rows = rows * chips
    local_grad = grads[:, :, 0, :]
    grad_float = grads.astype(jnp.float32)
    adam_m_new = 0.9 * adam_m + 0.1 * grad_float
    adam_v_new = 0.99 * adam_v + 0.01 * grad_float * grad_float
    adam_step = (adam_m_new / (jnp.sqrt(adam_v_new) + 1e-08))[:, :, 0, :]
    adam_part = kind_sums(adam_step * adam_step, widths, starts)
    adam_total = lax.psum(adam_part, ("fsdp", "tp"))
    outgoing = jnp.zeros((chips, rows, capacity), jnp.bfloat16)
    for kind in range(7):
        outgoing = outgoing.at[owner[:, kind], :, : widths[kind]].set(
            local_grad[:, :, starts[kind] : starts[kind] + widths[kind]]
        )
    arrived = lax.all_to_all(outgoing, "fsdp", split_axis=0, concat_axis=0, tiled=True)
    gathered = arrived.reshape(model_rows, capacity)
    chip_index = lax.axis_index("fsdp")
    matches = owner == chip_index
    owned = jnp.any(matches)
    width_class = jnp.where(owned, jnp.sum(jnp.where(matches, class_table[None, :], 0)), 1)
    stat_slot = stats[0]
    root_slot = roots[0]

    def stat_term_rows():

        def make_rows(wide):

            def branch():
                block = gathered[:, :wide]
                return gram_rows(block, gathered[:, :wide])

            return branch

        return lax.switch(width_class, [make_rows(wide) for wide in classes])

    stat_term = lax.psum_scatter(stat_term_rows(), "tp", scatter_dimension=0, tiled=True)

    def apply_rows(piece):

        def make_apply(wide):

            def branch():
                result = jnp.dot(piece, gathered[:, :wide], preferred_element_type=jnp.float32)
                return jnp.pad(result, ((0, 0), (0, capacity - wide)))

            return branch

        return lax.switch(width_class, [make_apply(wide) for wide in classes])

    precond = apply_rows(lax.all_gather(root_slot, "tp", axis=0, tiled=True)).astype(jnp.bfloat16)
    stats_new = jnp.where(owned, 0.9 * stat_slot + 0.1 * stat_term, stat_slot)[None]
    returned = lax.all_to_all(
        precond.reshape(chips, rows, capacity), "fsdp", split_axis=0, concat_axis=0, tiled=True
    )
    pieces = [returned[owner[:, kind], :, : widths[kind]] for kind in range(7)]
    direction = jnp.concatenate(pieces, axis=2).astype(jnp.float32)
    shampoo_part = kind_sums(direction * direction, widths, starts)
    shampoo_total = lax.psum(shampoo_part, ("fsdp", "tp"))
    ratio = jnp.sqrt(adam_total) / (jnp.sqrt(shampoo_total) + 1e-06)
    column_scale = jnp.concatenate(
        [jnp.broadcast_to(ratio[:, kind : kind + 1], (layers, widths[kind])) for kind in range(7)],
        axis=1,
    )
    weights_new = weights - 0.02 * (direction * column_scale[:, None, :])[:, :, None, :]
    vec_float = vec_grad.astype(jnp.float32)
    vec_m_new = 0.9 * vec_m + 0.1 * vec_float
    vec_v_new = 0.99 * vec_v + 0.01 * vec_float * vec_float
    vec_weight_new = vec_weight - 0.02 * vec_m_new / (jnp.sqrt(vec_v_new) + 1e-08)
    return (weights_new, adam_m_new, adam_v_new, stats_new, vec_weight_new, vec_m_new, vec_v_new)


def solution(mesh):
    placed = (
        P(),
        P(None, "fsdp", "tp", None),
        P(None, "fsdp", "tp", None),
        P(None, "fsdp", "tp", None),
        P(None, "fsdp", "tp", None),
        P("fsdp", "tp", None),
        P("fsdp", "tp", None),
        P(None, ("fsdp", "tp")),
        P(None, ("fsdp", "tp")),
        P(None, ("fsdp", "tp")),
        P(None, ("fsdp", "tp")),
    )
    return jax.shard_map(
        on_device,
        mesh=mesh,
        in_specs=placed,
        out_specs=(
            P(None, "fsdp", "tp", None),
            P(None, "fsdp", "tp", None),
            P(None, "fsdp", "tp", None),
            P("fsdp", "tp", None),
            P(None, ("fsdp", "tp")),
            P(None, ("fsdp", "tp")),
            P(None, ("fsdp", "tp")),
        ),
        check_vma=False,
    )
```

profile of v0, /device:TPU:0, one launch (start us, length us, event | category | flops | bytes accessed | tf_op | source)
XLA Modules:
  0.0 411.8 jit_solution(16580479824753953919)
XLA Ops:
  13.3 16.8 %while.4 = (s32[]{:T(128)}, bf16[16,56,2432]{2,1,0:T(8,128)(2,1)}, s32[2,2]{1,0:T(2,128)S(1)}, bf16[2,56,448]{2,1,0:T(8,128)(2,1)S(1)}, s32[]{:T(128)}, /*index=5*/s32[3]{0:T(128)S(1)}, s32[1]{0:T(128)}, s32[]{:T(128)}) while((s32[]{:T(128)}, bf16[16,56,2432]{2,1,0:T(8,128)(2,1)}, s32[2,2]{1,0:T(2,128)S(1)}, bf16[2,56,448]{2,1,0:T(8,128)(2,1)S(1)}, ...), condition=%wide.while_cond, body=%wide.while_body.sunk | while | flops 25107 | bytes 251051 | solution.py:61
  15.9 2.9 dynamic-slice_select_fusion.8
  18.8 2.9 dynamic-update-slice.12
  24.3 2.9 dynamic-slice_select_fusion.8
  27.2 2.9 dynamic-update-slice.12
  30.1 16.1 %while.5 = (s32[]{:T(128)}, bf16[16,56,2432]{2,1,0:T(8,128)(2,1)}, s32[2,2]{1,0:T(2,128)S(1)}, bf16[2,56,64]{2,1,0:T(8,128)(2,1)S(1)}, s32[]{:T(128)}, /*index=5*/s32[3]{0:T(128)S(1)}, s32[1]{0:T(128)}, s32[]{:T(128)}) while((s32[]{:T(128)}, bf16[16,56,2432]{2,1,0:T(8,128)(2,1)}, s32[2,2]{1,0:T(2,128)S(1)}, bf16[2,56,64]{2,1,0:T(8,128)(2,1)S(1)}, ...), condition=%wide.while_cond.1, body=%wide.while_body.1.sunk | while | flops 3603 | bytes 36011 | solution.py:61
  46.2 16.1 %while.6 = (s32[]{:T(128)}, bf16[16,56,2432]{2,1,0:T(8,128)(2,1)}, s32[2,2]{1,0:T(2,128)S(1)}, bf16[2,56,64]{2,1,0:T(8,128)(2,1)S(1)}, s32[]{:T(128)}, /*index=5*/s32[3]{0:T(128)S(1)}, s32[1]{0:T(128)}, s32[]{:T(128)}) while((s32[]{:T(128)}, bf16[16,56,2432]{2,1,0:T(8,128)(2,1)}, s32[2,2]{1,0:T(2,128)S(1)}, bf16[2,56,64]{2,1,0:T(8,128)(2,1)S(1)}, ...), condition=%wide.while_cond.2, body=%wide.while_body.2.sunk | while | flops 3603 | bytes 36011 | solution.py:61
  62.2 16.8 %while.7 = (s32[]{:T(128)}, bf16[16,56,2432]{2,1,0:T(8,128)(2,1)}, s32[2,2]{1,0:T(2,128)S(1)}, bf16[2,56,448]{2,1,0:T(8,128)(2,1)S(1)}, s32[]{:T(128)}, /*index=5*/s32[3]{0:T(128)S(1)}, s32[1]{0:T(128)}, s32[]{:T(128)}) while((s32[]{:T(128)}, bf16[16,56,2432]{2,1,0:T(8,128)(2,1)}, s32[2,2]{1,0:T(2,128)S(1)}, bf16[2,56,448]{2,1,0:T(8,128)(2,1)S(1)}, ...), condition=%wide.while_cond.3, body=%wide.while_body.3.sunk | while | flops 25107 | bytes 251051 | solution.py:61
  64.8 2.9 dynamic-slice_select_fusion.11
  67.8 2.9 dynamic-update-slice.15
  73.2 2.9 dynamic-slice_select_fusion.11
  76.1 2.9 dynamic-update-slice.15
  86.3 8.5 %all-to-all-start = ((bf16[16,56,2432]{2,1,0:T(8,128)(2,1)}), bf16[16,56,2432]{2,1,0:T(8,128)(2,1)}, u32[]{:S(2)}, u32[]{:S(2)}) async-start(bf16[16,56,2432]{2,1,0:T(8,128)(2,1)} %scatter_fusion.2), calls=%async_computation | async-start | bytes 8716288 | tf_op jit(solution)/shard_map/all_to_all | solution.py:64
  98.0 10.3 %all-gather.3.cloned.1.call-done = bf16[1,896,896]{2,1,0:T(8,128)(2,1)} async-done(((bf16[1,448,896]{2,1,0:T(8,128)(2,1)}), bf16[1,896,896]{2,1,0:T(8,128)(2,1)}) %all-gather.3.cloned.1.call-update) | async-done | bytes 1605648 | tf_op jit(solution)/shard_map/all_gather | solution.py:99
  108.3 69.2 %all-to-all-done = bf16[16,56,2432]{2,1,0:T(8,128)(2,1)} async-done(((bf16[16,56,2432]{2,1,0:T(8,128)(2,1)}), bf16[16,56,2432]{2,1,0:T(8,128)(2,1)}, u32[]{:S(2)}, u32[]{:S(2)}) %all-to-all-start) | async-done | bytes 4358176 | tf_op jit(solution)/shard_map/all_to_all | solution.py:64
  177.5 9.9 %conditional.2 = (bf16[896,2432]{0,1:T(8,128)(2,1)}) conditional(s32[]{:T(128)} %clamp.4, (bf16[896,2432]{1,0:T(8,128)(2,1)}, bf16[896,896]{1,0:T(8,128)(2,1)}) %tuple.144, (bf16[896,2432]{1,0:T(8,128)(2,1)}, bf16[896,896]{1,0:T(8,128)(2,1)}) %tuple.145, (bf16[896,896]{1,0:T(8,128)(2,1)}, bf16[896,2432]{1,0:T(8,128)(2,1)}) %tuple.146), branch_computations={%region_9.0_spmd, %region_10.0_spmd, %region_11.0_spmd} | conditional | flops 3904897024 | bytes 10321928 | solution.py:97
  177.5 9.9 %fusion.27 = bf16[896,2432]{0,1:T(8,128)(2,1)} fusion(bf16[896,896]{1,0:T(8,128)(2,1)} %get-tuple-element.27, bf16[896,2432]{1,0:T(8,128)(2,1)} %get-tuple-element.28), kind=kOutput, calls=%fused_computation.96 | convolution fusion | flops 3904897024 | bytes 10321920 | tf_op jit(solution)/shard_map/cond/branch_2_fun/dot_general | solution.py:92
  187.4 7.1 %copy.72 = bf16[896,2432]{1,0:T(8,128)(2,1)} copy(bf16[896,2432]{0,1:T(8,128)(2,1)} %get-tuple-element.397) | data formatting | bytes 8716288 | tf_op jit(solution)/shard_map/cond | solution.py:97
  194.6 20.7 %all-to-all-start.1 = ((bf16[16,56,2432]{2,1,0:T(8,128)(2,1)}), bf16[16,56,2432]{2,1,0:T(8,128)(2,1)}, u32[]{:S(2)}, u32[]{:S(2)}) async-start(bf16[16,56,2432]{2,1,0:T(8,128)(2,1)} %bitcast.96), calls=%async_computation.1 | async-start | bytes 8716288 | tf_op jit(solution)/shard_map/all_to_all | solution.py:101
  215.4 10.3 %conditional.3 = (f32[896,896]{1,0:T(8,128)}) conditional(s32[]{:T(128)} %clamp.4, bf16[896,2432]{1,0:T(8,128)(2,1)} %bitcast.1, bf16[896,2432]{1,0:T(8,128)(2,1)} %bitcast.1, bf16[896,2432]{1,0:T(8,128)(2,1)} %bitcast.1), branch_computations={%region_28.29_spmd, %region_29.30_spmd, %region_30.31_spmd} | conditional | flops 3904897024 | bytes 7569416 | solution.py:83
  215.6 10.1 %fusion.28 = f32[896,896]{1,0:T(8,128)} fusion(bf16[896,2432]{1,0:T(8,128)(2,1)} %param.5), kind=kOutput, calls=%fused_computation.97 | convolution fusion | flops 3904897024 | bytes 7569408 | tf_op jit(solution)/shard_map/cond/branch_2_fun/dot_general | solution.py:35
  227.2 20.8 %divide_multiply_fusion = (f32[2,56,1,8320]{3,2,1,0:T(1,128)S(1)}, f32[2,56,1,8320]{3,2,1,0:T(1,128)}, f32[2,56,1,8320]{3,2,1,0:T(1,128)}) fusion(bf16[2,56,1,8320]{3,1,2,0:T(8,128)(2,1)S(1)} %copy-done.1, f32[2,56,1,8320]{3,2,1,0:T(1,128)} %param.22, f32[2,56,1,8320]{3,2,1,0:T(1,128)} %param.21), kind=kLoop, calls=%fused_computation.36 | loop fusion | flops 10250240 | bytes 20500480 | tf_op jit(solution)/shard_map/mul | solution.py:57
  255.2 3.4 fusion.10
  258.6 38.1 %all-to-all-done.1 = bf16[16,56,2432]{2,1,0:T(8,128)(2,1)} async-done(((bf16[16,56,2432]{2,1,0:T(8,128)(2,1)}), bf16[16,56,2432]{2,1,0:T(8,128)(2,1)}, u32[]{:S(2)}, u32[]{:S(2)}) %all-to-all-start.1) | async-done | bytes 4358176 | tf_op jit(solution)/shard_map/all_to_all | solution.py:101
  296.6 12.8 %copy.73 = bf16[16,56,2432]{1,0,2:T(8,128)(2,1)} copy(bf16[16,56,2432]{2,1,0:T(8,128)(2,1)} %all-to-all-done.1) | data formatting | bytes 8716288 | tf_op jit(solution)/shard_map/all_to_all | solution.py:101
  314.4 2.9 gather_fusion.3
  317.4 2.8 gather_fusion
  321.8 2.9 gather_fusion.4
  324.7 2.9 gather_fusion.5
  327.6 2.9 gather_fusion.6
  337.4 55.6 %all-reduce.6 = (f32[2,7]{1,0:T(2,128)S(1)}, f32[2,7]{1,0:T(2,128)S(1)}) all-reduce(f32[2,7]{1,0:T(2,128)S(1)} %stack.63, f32[2,7]{1,0:T(2,128)S(1)} %stack.55), channel_id=1, replica_groups=mesh['fsdp'=16,'tp'=2] {'fsdp','tp'}, use_global_device_ids=true, to_apply=%region_27.28 | all-reduce | flops 28 | bytes 224 | tf_op jit(solution)/shard_map/psum | solution.py:107
  399.3 5.7 %copy.101 = f32[2,56,1,8320]{3,2,1,0:T(1,128)} copy(f32[2,56,1,8320]{3,1,0,2:T(8,128)S(1)} %copy_subtract_fusion) | data formatting | bytes 7454720
  (135 shorter events, 86.2 us)
Async XLA Ops:
  7.2 3.5 copy-start.9
  9.1 4.2 %copy-start.10 = (s32[3]{0:T(128)S(1)}, s32[3]{0:T(128)}, u32[]{:S(2)}) copy-start(s32[3]{0:T(128)} %constant.291) | copy-start | bytes 40
  10.6 19.4 %copy-start.11 = (s32[3]{0:T(128)S(1)}, s32[3]{0:T(128)}, u32[]{:S(2)}) copy-start(s32[3]{0:T(128)} %constant.305) | copy-start | bytes 40
  86.3 9.9 %copy-start.15 = (s32[7]{0:T(128)S(1)}, s32[7]{0:T(128)}, u32[]{:S(2)}) copy-start(s32[7]{0:T(128)} %constant.14.clone) | copy-start | bytes 88
  86.3 91.2 %all-to-all-start = ((bf16[16,56,2432]{2,1,0:T(8,128)(2,1)}), bf16[16,56,2432]{2,1,0:T(8,128)(2,1)}, u32[]{:S(2)}, u32[]{:S(2)}) async-start(bf16[16,56,2432]{2,1,0:T(8,128)(2,1)} %scatter_fusion.2), calls=%async_computation | async-start | bytes 8716288 | tf_op jit(solution)/shard_map/all_to_all | solution.py:64
  94.8 13.5 %all-gather.3.cloned.1.call-start = ((), (), s32[]{:S(2)}) async-start(), calls=%async_computation.4 | async-start | bytes 2408448 | tf_op jit(solution)/shard_map/all_gather | solution.py:99
  194.6 102.1 %all-to-all-start.1 = ((bf16[16,56,2432]{2,1,0:T(8,128)(2,1)}), bf16[16,56,2432]{2,1,0:T(8,128)(2,1)}, u32[]{:S(2)}, u32[]{:S(2)}) async-start(bf16[16,56,2432]{2,1,0:T(8,128)(2,1)} %bitcast.96), calls=%async_computation.1 | async-start | bytes 8716288 | tf_op jit(solution)/shard_map/all_to_all | solution.py:101
  215.3 39.9 %reduce-scatter.2.cloned.1.call-start = ((), (), s32[]{:S(2)}) async-start(), calls=%async_computation.3 | async-start | bytes 4816896 | tf_op jit(solution)/shard_map/reduce_scatter | solution.py:85
  225.6 1.5 copy-start.1
  248.2 1.9 copy-start
  248.3 6.3 %copy-start.12 = (f32[2,92]{1,0:T(2,128)S(1)}, f32[2,92]{1,0:T(2,128)}, u32[]{:S(2)}) copy-start(f32[2,92]{1,0:T(2,128)} %param.25) | copy-start | bytes 2212
  248.3 6.3 %copy-start.13 = (f32[2,92]{1,0:T(2,128)S(1)}, f32[2,92]{1,0:T(2,128)}, u32[]{:S(2)}) copy-start(f32[2,92]{1,0:T(2,128)} %param.27) | copy-start | bytes 2212
  248.3 6.3 %copy-start.14 = (f32[2,92]{1,0:T(2,128)S(1)}, f32[2,92]{1,0:T(2,128)}, u32[]{:S(2)}) copy-start(f32[2,92]{1,0:T(2,128)} %param.28) | copy-start | bytes 2212
  248.3 6.3 %copy-start.16 = (bf16[2,92]{1,0:T(2,128)(2,1)S(1)}, bf16[2,92]{1,0:T(2,128)(2,1)}, u32[]{:S(2)}) copy-start(bf16[2,92]{1,0:T(2,128)(2,1)} %param.26) | copy-start | bytes 1108
  248.3 6.9 %copy-start.2 = (f32[1,448,896]{2,1,0:T(8,128)S(1)}, f32[1,448,896]{2,1,0:T(8,128)}, u32[]{:S(2)}) copy-start(f32[1,448,896]{2,1,0:T(8,128)} %param.23) | copy-start | bytes 4816900
  313.7 3.6 copy-start.7
  317.4 10.2 %copy-start.5 = (bf16[2,56,448]{1,0,2:T(2,128)(2,1)}, bf16[2,56,448]{1,0,2:T(2,128)(2,1)S(1)}, u32[]{:S(2)}) copy-start(bf16[2,56,448]{1,0,2:T(2,128)(2,1)S(1)} %gather_fusion.3) | copy-start | bytes 301060
  320.2 7.3 %copy-start.3 = (bf16[2,56,448]{1,0,2:T(2,128)(2,1)}, bf16[2,56,448]{1,0,2:T(2,128)(2,1)S(1)}, u32[]{:S(2)}) copy-start(bf16[2,56,448]{1,0,2:T(2,128)(2,1)S(1)} %gather_fusion) | copy-start | bytes 301060
  333.5 1.5 copy-start.8
  333.5 1.6 copy-start.6
  333.5 3.1 copy-start.4
Sparse Core Ops, SparseCore 0:
  97.2 11.0 all-gather.2
  225.8 12.2 reduce-scatter.1
where the time goes:
time: 415 us; the launch traced here: 412 us
  waiting for transfers between devices  118 us (28%)
  local copies, waits for them, and re-layouts  100 us (24%)
  other arithmetic  72.3 us (17%)
  blocking collectives  55.6 us (13%)
  starting transfers between devices  29.3 us (7%)
  matrix products  20 us (5%)
  between operations  15.6 us (4%)
    all_to_all x1, waiting for transfers between devices, on_device(): lax.all_to_all(outgoing, 'fsdp', split_axis=0, concat_axis=0, tiled=True)  69.2 us
    psum x1, blocking collectives, on_device(): shampoo_total = lax.psum(shampoo_part, ('fsdp', 'tp'))  55.6 us
    scatter x16, other arithmetic  38.8 us
    all_to_all x1, waiting for transfers between devices, on_device(): lax.all_to_all(precond.reshape(chips, rows, capacity), 'fsdp', split_axis...  38.1 us
    scatter x24, local copies, waits for them, and re-layouts  26.9 us
    gather x11, local copies, waits for them, and re-layouts, on_device(): pieces = [returned[owner[:, kind], :, :widths[kind]] for kind in range(7)]  20.9 us
    mul x1, other arithmetic, on_device(): adam_part = kind_sums(adam_step * adam_step, widths, starts)  20.8 us
    all_to_all x1, starting transfers between devices, on_device(): lax.all_to_all(precond.reshape(chips, rows, capacity), 'fsdp', split_axis...  20.7 us
  transfers between devices with their start and end apart: 4, of which 3 were waited for; matrix products, arithmetic and copies ran while one was open for 10% of the time, Pallas kernels for 0%

commit v1 on v0

v1 whole, which is shorter than its diff:
```python
import jax
import jax.numpy as jnp
from jax import lax
from jax.experimental import pallas as pl
from jax.experimental.pallas import tpu as pltpu
from jax.sharding import PartitionSpec as P

FF = 4864
QW = 896
KW = 128
LANES = 128
WIDTHS = [QW // 2, KW // 2, KW // 2, QW // 2, FF // 2, FF // 2, FF // 2]
STARTS = [sum(WIDTHS[:kind]) for kind in range(7)]
TILE0 = [start // LANES for start in STARTS]
TILES = [-(-(start + wide) // LANES) - start // LANES for start, wide in zip(STARTS, WIDTHS)]
CAP = max(TILES)
HALF = sum(WIDTHS)
ALL_TILES = HALF // LANES


def row_block(rows):
    return 8 if rows % 8 == 0 else rows


def send_kernel(layer_ref, tile_ref, low_ref, high_ref, grad_ref, out_ref):
    slot = pl.program_id(0)
    layer = layer_ref[slot]
    first = tile_ref[slot]
    low = low_ref[slot]
    high = high_ref[slot]
    lane = lax.broadcasted_iota(jnp.int32, (grad_ref.shape[1], LANES), 1)
    for tile in range(CAP):
        at = jnp.minimum(first + tile, ALL_TILES - 1)
        piece = grad_ref[layer, :, pl.ds(pl.multiple_of(at * LANES, LANES), LANES)]
        column = lane + (first + tile) * LANES
        keep = (column >= low) & (column < high)
        out_ref[0, :, tile * LANES : (tile + 1) * LANES] = jnp.where(
            keep, piece.astype(jnp.float32), 0.0
        ).astype(jnp.bfloat16)


def build_send(grads, slot_layer, slot_kind):
    layers, rows, _ = grads.shape
    chips = slot_layer.shape[0]
    tile0 = jnp.array(TILE0 + [0], jnp.int32)[slot_kind]
    low = jnp.array(STARTS + [0], jnp.int32)[slot_kind]
    high = jnp.array([s + w for s, w in zip(STARTS, WIDTHS)] + [0], jnp.int32)[slot_kind]
    return pl.pallas_call(
        send_kernel,
        out_shape=jax.ShapeDtypeStruct((chips, rows, CAP * LANES), jnp.bfloat16),
        grid_spec=pltpu.PrefetchScalarGridSpec(
            num_scalar_prefetch=4,
            grid=(chips,),
            in_specs=[pl.BlockSpec((layers, rows, HALF), lambda i, *_: (0, 0, 0))],
            out_specs=pl.BlockSpec((1, rows, CAP * LANES), lambda i, *_: (i, 0, 0)),
        ),
        name="build_send",
    )(slot_layer, tile0, low, high, grads)


def update_kernel(owner_ref, scale_ref, weight_ref, *refs):
    pieces = refs[:7]
    out_ref = refs[7]
    layer = pl.program_id(0)
    rows = pieces[0].shape[1]
    lane = lax.broadcasted_iota(jnp.int32, (rows, LANES), 1)
    for tile in range(ALL_TILES):
        step = None
        for kind in range(7):
            at = tile - TILE0[kind]
            if not 0 <= at < TILES[kind]:
                continue
            piece = pieces[kind][0, :, at * LANES : (at + 1) * LANES].astype(jnp.float32)
            piece = 0.02 * (scale_ref[layer, kind] * piece)
            low = STARTS[kind] - tile * LANES
            if step is not None:
                step = jnp.where(lane >= low, piece, step)
            else:
                step = piece
        where = pl.ds(tile, rows, stride=ALL_TILES)
        out_ref[0, where, :] = weight_ref[0, where, :] - step


def update_weights(owner, ratio, weights, returned):
    layers, rows = weights.shape[:2]
    block = row_block(rows)
    blocks = rows // block
    view = (layers * blocks, block * ALL_TILES, LANES)

    def piece_spec(kind):
        wide = TILES[kind] * LANES
        return pl.BlockSpec((1, block, wide), lambda l, r, owner, scale: (owner[l, kind], r, 0))

    flat_spec = pl.BlockSpec((1,) + view[1:], lambda l, r, owner, scale: (l * blocks + r, 0, 0))
    out = pl.pallas_call(
        update_kernel,
        out_shape=jax.ShapeDtypeStruct(view, jnp.float32),
        grid_spec=pltpu.PrefetchScalarGridSpec(
            num_scalar_prefetch=2,
            grid=(layers, blocks),
            in_specs=[flat_spec] + [piece_spec(kind) for kind in range(7)],
            out_specs=flat_spec,
        ),
        name="update_weights",
    )(owner, ratio, weights.reshape(view), *[returned] * 7)
    return out.reshape(weights.shape)


def kind_sums(values):
    return jnp.stack(
        [
            jnp.sum(values[:, :, start : start + wide], axis=(1, 2))
            for start, wide in zip(STARTS, WIDTHS)
        ],
        axis=1,
    )


def swap_cores(value):
    return lax.ppermute(value, "tp", [(0, 1), (1, 0)])


def on_device(
    owner, grads, weights, adam_m, adam_v, stats, roots, vec_weight, vec_grad, vec_m, vec_v
):
    chips = lax.axis_size("fsdp")
    chip = lax.axis_index("fsdp")
    core = lax.axis_index("tp")
    layers = grads.shape[0]
    rows = grads.shape[1]
    model_rows = rows * chips
    half_rows = model_rows // 2
    flat_owner = owner.reshape(-1)
    named = flat_owner[None, :] == jnp.arange(chips, dtype=jnp.int32)[:, None]
    order = jnp.arange(layers * 7, dtype=jnp.int32)[None, :]
    matrix = jnp.sum(jnp.where(named, order, 0), axis=1)
    has = jnp.any(named, axis=1)
    slot_layer = matrix // 7
    slot_kind = jnp.where(has, matrix % 7, 7)
    owned = has[chip]

    outgoing = build_send(grads[:, :, 0, :], slot_layer, slot_kind)
    arrived = lax.all_to_all(outgoing, "fsdp", split_axis=0, concat_axis=0, tiled=True)
    gathered = arrived.reshape(model_rows, CAP * LANES)

    root_mine = roots[0]
    root_other = swap_cores(root_mine)
    root = jnp.where(
        core == 0,
        jnp.concatenate([root_mine, root_other]),
        jnp.concatenate([root_other, root_mine]),
    )

    grad_float = grads.astype(jnp.float32)
    adam_m_new = 0.9 * adam_m + 0.1 * grad_float
    adam_v_new = 0.99 * adam_v + 0.01 * grad_float * grad_float
    adam_step = (adam_m_new / (jnp.sqrt(adam_v_new) + 1e-08))[:, :, 0, :]
    adam_part = kind_sums(adam_step * adam_step)

    precond = jnp.dot(root, gathered, preferred_element_type=jnp.float32).astype(jnp.bfloat16)
    returned = lax.all_to_all(
        precond.reshape(chips, rows, CAP * LANES), "fsdp", split_axis=0, concat_axis=0, tiled=True
    )
    precond_float = precond.astype(jnp.float32)
    shampoo_part = jnp.sum(precond_float * precond_float)
    mine = jnp.where(named[chip], shampoo_part, 0.0).reshape(layers, 7)
    adam_total, shampoo_total = lax.psum((adam_part, mine), ("fsdp", "tp"))
    ratio = jnp.sqrt(adam_total) / (jnp.sqrt(shampoo_total) + 1e-06)

    gram = lax.dot_general(
        gathered, gathered, (((1,), (1,)), ((), ())), preferred_element_type=jnp.float32
    )
    top = gram[:half_rows]
    bottom = gram[half_rows:]
    keep = jnp.where(core == 0, top, bottom)
    give = jnp.where(core == 0, bottom, top)
    stat_term = keep + swap_cores(give)
    stats_new = jnp.where(owned, 0.9 * stats[0] + 0.1 * stat_term, stats[0])[None]

    weights_new = update_weights(owner, ratio, weights, returned)

    vec_float = vec_grad.astype(jnp.float32)
    vec_m_new = 0.9 * vec_m + 0.1 * vec_float
    vec_v_new = 0.99 * vec_v + 0.01 * vec_float * vec_float
    vec_weight_new = vec_weight - 0.02 * vec_m_new / (jnp.sqrt(vec_v_new) + 1e-08)
    return (weights_new, adam_m_new, adam_v_new, stats_new, vec_weight_new, vec_m_new, vec_v_new)


def solution(mesh):
    matrix = P(None, "fsdp", "tp", None)
    slot = P("fsdp", "tp", None)
    vector = P(None, ("fsdp", "tp"))
    return jax.shard_map(
        on_device,
        mesh=mesh,
        in_specs=(P(), matrix, matrix, matrix, matrix, slot, slot, vector, vector, vector, vector),
        out_specs=(matrix, matrix, matrix, slot, vector, vector, vector),
        check_vma=False,
    )
```

time: 415 us -> 272 us (0.66)
  local copies, waits for them, and re-layouts: 100 us -> 12.6 us
  other arithmetic: 72.3 us -> 31.3 us
  waiting for transfers between devices: 118 us -> 82.6 us
  blocking collectives: 55.6 us -> 76.4 us
  Pallas kernels: 0 us -> 18.9 us
  between operations: 15.6 us -> 0.78 us
    scatter x16 -> x0, other arithmetic: 38.8 us -> none
    all_to_all x1, waiting for transfers between devices: 38.1 us -> 0.01 us  [on_device(): lax.all_to_all(precond.reshape(chips, rows, CAP * LANES), 'fsdp', split_a...]
    scatter x27 -> x0, local copies, waits for them, and re-layouts: 34.2 us -> none
    psum x1, blocking collectives: 55.6 us -> 76.4 us  [on_device(): adam_total, shampoo_total = lax.psum((adam_part, mine), ('fsdp', 'tp'))]
    pallas_call x0 -> x2, Pallas kernels: none -> 18.9 us  [the longest x1 10.3 us: update_weights(): pl.pallas_call(update_kernel, out_shape=jax.ShapeDtypeStruct(view, jnp.fl...]
    gather x11 -> x3, local copies, waits for them, and re-layouts: 20.9 us -> 5.48 us  [the longest x1 1.83 us: build_send(): jnp.array([s + w for s, w in zip(STARTS, WIDTHS)] + [0], jnp.int32)]
    all_to_all x1 -> x0, local copies, waits for them, and re-layouts: 12.8 us -> none  [on_device(): lax.all_to_all(precond.reshape(chips, rows, capacity), 'fsdp', split_axis...]
    all_to_all x1, waiting for transfers between devices: 69.2 us -> 80.3 us  [on_device(): lax.all_to_all(outgoing, 'fsdp', split_axis=0, concat_axis=0, tiled=True)]
  transfers between devices with their start and end apart: 4 -> 4, of which waited for: 3 -> 2; matrix products, arithmetic and copies ran while one was open for 10% -> 16% of each run, Pallas kernels for 0% -> 0%
where the time goes in v1:
time: 272 us; the launch traced here: 271 us
  waiting for transfers between devices  82.6 us (30%)
  blocking collectives  76.4 us (28%)
  other arithmetic  31.3 us (12%)
  starting transfers between devices  29.3 us (11%)
  matrix products  19.1 us (7%)
  Pallas kernels  18.9 us (7%)
  local copies, waits for them, and re-layouts  12.6 us (5%)
    all_to_all x1, waiting for transfers between devices, on_device(): lax.all_to_all(outgoing, 'fsdp', split_axis=0, concat_axis=0, tiled=True)  80.3 us
    psum x1, blocking collectives, on_device(): adam_total, shampoo_total = lax.psum((adam_part, mine), ('fsdp', 'tp'))  76.4 us
    all_to_all x1, starting transfers between devices, on_device(): lax.all_to_all(precond.reshape(chips, rows, CAP * LANES), 'fsdp', split_a...  20.7 us
    mul x1, other arithmetic, on_device(): adam_part = kind_sums(adam_step * adam_step)  19.8 us
    dot_general x1, matrix products, on_device(): jnp.dot(root, gathered, preferred_element_type=jnp.float32)  10.5 us
    pallas_call x1, Pallas kernels, update_weights(): pl.pallas_call(update_kernel, out_shape=jax.ShapeDtypeStruct(view, jnp.fl...  10.3 us
    dot_general x1, matrix products, on_device(): lax.dot_general(gathered, gathered, (((1,), (1,)), ((), ())), preferred_e...  8.57 us
    pallas_call x1, Pallas kernels, build_send(): pl.pallas_call(send_kernel, out_shape=jax.ShapeDtypeStruct((chips, rows,...  8.57 us
  transfers between devices with their start and end apart: 4, of which 2 were waited for; matrix products, arithmetic and copies ran while one was open for 16% of the time, Pallas kernels for 0%

profile of v1, /device:TPU:0, one launch (start us, length us, event | category | flops | bytes accessed | tf_op | source)
XLA Modules:
  0.0 270.9 jit_solution(1200508955909861047)
XLA Ops:
  0.6 0.8 eq.22
  1.4 0.1 select_reduce_fusion
  1.5 0.1 fusion.9
  1.6 0.5 and_select_fusion.1.layer_ref
  2.2 1.8 gather_fusion.2
  4.0 1.8 gather_fusion.1
  5.8 1.8 gather_fusion
  7.7 8.6 %build_send.1 = bf16[16,56,2432]{2,1,0:T(8,128)(2,1)} custom-call(s32[16]{0:T(128)} %and_select_fusion.1.layer_ref, s32[16]{0:T(128)} %gather_fusion, s32[16]{0:T(128)} %gather_fusion.1, s32[16]{0:T(128)} %gather_fusion.2, bf16[2,56,8320]{2,1,0:T(8,128)(2,1)} %bitcast.44), custom_call_target="tpu_custom_call" | custom-call | tf_op jit(solution)/shard_map/build_send/pallas_call | solution.py:48
  16.2 8.5 %all-to-all-start = ((bf16[16,56,2432]{2,1,0:T(8,128)(2,1)}), bf16[16,56,2432]{2,1,0:T(8,128)(2,1)}, u32[]{:S(2)}, u32[]{:S(2)}) async-start(bf16[16,56,2432]{2,1,0:T(8,128)(2,1)} %build_send.1), calls=%async_computation | async-start | bytes 8716288 | tf_op jit(solution)/shard_map/all_to_all | solution.py:143
  24.8 2.3 collective-permute-done
  27.1 80.3 %all-to-all-done = bf16[16,56,2432]{2,1,0:T(8,128)(2,1)} async-done(((bf16[16,56,2432]{2,1,0:T(8,128)(2,1)}), bf16[16,56,2432]{2,1,0:T(8,128)(2,1)}, u32[]{:S(2)}, u32[]{:S(2)}) %all-to-all-start) | async-done | bytes 4358176 | tf_op jit(solution)/shard_map/all_to_all | solution.py:143
  107.5 10.5 %multiply_reduce_fusion = (f32[]{:T(128)}, bf16[896,2432]{1,0:T(8,128)(2,1)}) fusion(bf16[896,2432]{1,0:T(8,128)(2,1)} %bitcast.12, bf16[448,896]{1,0:T(8,128)(2,1)S(1)} %collective-permute-done, bf16[448,896]{1,0:T(8,128)(2,1)S(1)} %bitcast.56, pred[]{:T(512)S(6)} %eq.26), kind=kOutput, calls=%fused_computation.3 | convolution fusion | flops 3920838656 | bytes 10321925 | tf_op jit(solution)/shard_map/dot_general | solution.py:160
  117.9 20.7 %all-to-all-start.1 = ((bf16[16,56,2432]{2,1,0:T(8,128)(2,1)}), bf16[16,56,2432]{2,1,0:T(8,128)(2,1)}, u32[]{:S(2)}, u32[]{:S(2)}) async-start(bf16[16,56,2432]{2,1,0:T(8,128)(2,1)} %bitcast.45), calls=%async_computation.1 | async-start | bytes 8716288 | tf_op jit(solution)/shard_map/all_to_all | solution.py:161
  138.7 8.6 %fusion.18 = f32[896,896]{1,0:T(8,128)S(1)} fusion(bf16[896,2432]{1,0:T(8,128)(2,1)} %bitcast.12), kind=kOutput, calls=%fused_computation.48 | convolution fusion | flops 3904897024 | bytes 7569408 | tf_op jit(solution)/shard_map/dot_general | solution.py:170
  147.3 1.3 slice_select_fusion
  148.7 0.7 copy-done.1
  149.4 19.8 %divide_multiply_fusion = (f32[2,56,1,8320]{3,2,1,0:T(1,128)}, f32[2,56,1,8320]{3,2,1,0:T(1,128)}, f32[2,56,1,8320]{3,2,1,0:T(1,128)}) fusion(bf16[2,56,1,8320]{3,1,2,0:T(8,128)(2,1)S(1)} %copy-done.1, f32[2,56,1,8320]{3,2,1,0:T(1,128)S(1)} %copy-done.2, f32[2,56,1,8320]{3,2,1,0:T(1,128)S(1)} %copy-done.3), kind=kLoop, calls=%fused_computation.9 | loop fusion | flops 10250240 | bytes 20500480 | tf_op jit(solution)/shard_map/mul | solution.py:158
  169.2 2.3 copy.48
  171.5 1.8 copy-done
  173.3 0.2 slice_reduce_fusion.5
  173.5 0.1 copy.32
  173.7 1.2 slice_reduce_fusion.3
  175.1 2.2 slice_reduce_fusion
  177.3 0.1 copy.36
  177.6 0.1 stack.31
  177.7 0.6 divide_subtract_fusion
  178.3 0.6 fusion.12
  179.0 0.6 dynamic_slice.7
  179.6 76.4 %all-reduce = (f32[2,7]{1,0:T(2,128)S(1)}, f32[2,7]{1,0:T(2,128)S(1)}) all-reduce(f32[2,7]{1,0:T(2,128)S(1)} %select_n.93, f32[2,7]{1,0:T(2,128)S(1)} %stack.31), channel_id=1, replica_groups=mesh['fsdp'=16,'tp'=2] {'fsdp','tp'}, use_global_device_ids=true, to_apply=%region_11.12 | all-reduce | flops 28 | bytes 224 | tf_op jit(solution)/shard_map/psum | solution.py:167
  256.0 0.6 add_divide_fusion.scale_ref
  256.6 4.0 %fusion.7 = f32[1,448,896]{2,1,0:T(8,128)} fusion(f32[1,448,896]{2,1,0:T(8,128)} %param.19, f32[448,896]{1,0:T(8,128)} %collective-permute-done.1, f32[896,896]{1,0:T(8,128)S(1)} %fusion.18, pred[]{:T(512)S(6)} %eq.26, pred[]{:T(512)} %bitcast.16), kind=kLoop, calls=%fused_computation.20 | loop fusion | flops 2408448 | bytes 8028162 | tf_op jit(solution)/shard_map/broadcast_in_dim | solution.py:178
  260.6 10.3 %update_weights.1 = f32[14,520,128]{2,1,0:T(8,128)} custom-call(s32[2,7]{1,0:T(2,128)} %owner_ref.1, f32[2,7]{1,0:T(2,128)} %add_divide_fusion.scale_ref, f32[14,520,128]{2,1,0:T(8,128)} %bitcast.46, bf16[16,56,2432]{2,1,0:T(8,128)(2,1)} %all-to-all-done.1.refs_0_.refs_1_.refs_2_.refs_3_.refs_4_.refs_5_.refs_6_, ...), custom_call_target="tpu_custom_call" | custom-call | tf_op jit(solution)/shard_map/update_weights/pallas_call | solution.py:95
  (28 shorter events, 0.7 us)
Async XLA Ops:
  16.2 8.5 %copy-start.8 = (bf16[1,448,896]{2,1,0:T(8,128)(2,1)S(1)}, bf16[1,448,896]{2,1,0:T(8,128)(2,1)}, u32[]{:S(2)}) copy-start(bf16[1,448,896]{2,1,0:T(8,128)(2,1)} %param.20) | copy-start | bytes 2408452
  16.2 91.2 %all-to-all-start = ((bf16[16,56,2432]{2,1,0:T(8,128)(2,1)}), bf16[16,56,2432]{2,1,0:T(8,128)(2,1)}, u32[]{:S(2)}, u32[]{:S(2)}) async-start(bf16[16,56,2432]{2,1,0:T(8,128)(2,1)} %build_send.1), calls=%async_computation | async-start | bytes 8716288 | tf_op jit(solution)/shard_map/all_to_all | solution.py:143
  24.7 2.4 collective-permute-start
  117.9 142.7 %all-to-all-start.1 = ((bf16[16,56,2432]{2,1,0:T(8,128)(2,1)}), bf16[16,56,2432]{2,1,0:T(8,128)(2,1)}, u32[]{:S(2)}, u32[]{:S(2)}) async-start(bf16[16,56,2432]{2,1,0:T(8,128)(2,1)} %bitcast.45), calls=%async_computation.1 | async-start | bytes 8716288 | tf_op jit(solution)/shard_map/all_to_all | solution.py:161
  138.7 9.9 %copy-start.2 = (f32[2,56,1,8320]{3,2,1,0:T(1,128)S(1)}, f32[2,56,1,8320]{3,2,1,0:T(1,128)}, u32[]{:S(2)}) copy-start(f32[2,56,1,8320]{3,2,1,0:T(1,128)} %param.18) | copy-start | bytes 11182084
  138.7 9.9 %copy-start.3 = (f32[2,56,1,8320]{3,2,1,0:T(1,128)S(1)}, f32[2,56,1,8320]{3,2,1,0:T(1,128)}, u32[]{:S(2)}) copy-start(f32[2,56,1,8320]{3,2,1,0:T(1,128)} %param.17) | copy-start | bytes 11182084
  147.3 2.1 copy-start.1
  148.6 107.9 %collective-permute-start.1 = (f32[448,896]{1,0:T(8,128)}, f32[448,896]{1,0:T(8,128)}, u32[]{:S(2)}, u32[]{:S(2)}) collective-permute-start(f32[448,896]{1,0:T(8,128)} %slice_select_fusion), channel_id=1, source_target_pairs={{0,1},{1,0},{2,3},{3,2},{4,5},{5,4},{6,7},{7,6},{8,9},{9,8},{10,11... | collective-permute-start | bytes 4816904 | tf_op jit(solution)/shard_map/ppermute | solution.py:120
  171.4 1.9 copy-start
  171.5 6.3 %copy-start.4 = (f32[2,92]{1,0:T(2,128)S(1)}, f32[2,92]{1,0:T(2,128)}, u32[]{:S(2)}) copy-start(f32[2,92]{1,0:T(2,128)} %param.21) | copy-start | bytes 2212
  171.5 6.3 %copy-start.5 = (f32[2,92]{1,0:T(2,128)S(1)}, f32[2,92]{1,0:T(2,128)}, u32[]{:S(2)}) copy-start(f32[2,92]{1,0:T(2,128)} %param.23) | copy-start | bytes 2212
  171.5 6.2 %copy-start.6 = (f32[2,92]{1,0:T(2,128)S(1)}, f32[2,92]{1,0:T(2,128)}, u32[]{:S(2)}) copy-start(f32[2,92]{1,0:T(2,128)} %param.24) | copy-start | bytes 2212
  171.5 6.2 %copy-start.7 = (bf16[2,92]{1,0:T(2,128)(2,1)S(1)}, bf16[2,92]{1,0:T(2,128)(2,1)}, u32[]{:S(2)}) copy-start(bf16[2,92]{1,0:T(2,128)(2,1)} %param.22) | copy-start | bytes 1108

commit v2 on v1

v2 whole, which is shorter than its diff:
```python
import functools

import jax
import jax.numpy as jnp
from jax import lax
from jax.experimental import pallas as pl
from jax.experimental.pallas import tpu as pltpu
from jax.sharding import PartitionSpec as P

FF = 4864
QW = 896
KW = 128
LANES = 128
WIDTHS = [QW // 2, KW // 2, KW // 2, QW // 2, FF // 2, FF // 2, FF // 2]
STARTS = [sum(WIDTHS[:kind]) for kind in range(7)]
TILE0 = [start // LANES for start in STARTS]
TILES = [-(-(start + wide) // LANES) - start // LANES for start, wide in zip(STARTS, WIDTHS)]
HALF = sum(WIDTHS)
ALL_TILES = HALF // LANES
GROUP = 4
WIDE = -(-max(TILES) // GROUP)
FIRST_WIDE = 4
NONE = 7


def pick(index, values):
    result = jnp.int32(values[-1])
    for at in range(len(values) - 1):
        result = jnp.where(index == at, values[at], result)
    return result


def rank_tile(rank, wide_ranks):
    return jnp.where(rank < wide_ranks, rank * WIDE, wide_ranks * (WIDE - 1) + rank)


def slot_tiles(wide_ranks):
    return wide_ranks * WIDE + GROUP - wide_ranks


def plan_kernel(owner_ref, layer_ref, kind_ref, place_ref, base_ref, rank_ref, level_ref, mat_ref):
    layers = owner_ref.shape[0]
    chips = layer_ref.shape[0]

    def clear(chip, carry):
        mat_ref[chip] = -1
        return carry

    lax.fori_loop(0, chips, clear, 0)

    def name(matrix, carry):
        mat_ref[owner_ref[matrix // 7, matrix % 7]] = matrix
        return carry

    lax.fori_loop(0, layers * 7, name, 0)

    def rank_group(group, level):
        first = group * GROUP
        mats = [mat_ref[first + i] for i in range(GROUP)]
        wide = [((m >= 0) & (m % 7 >= FIRST_WIDE)).astype(jnp.int32) for m in mats]
        count = sum(wide)
        before_wide = jnp.int32(0)
        before_rest = count
        for i in range(GROUP):
            rank = jnp.where(wide[i] == 1, before_wide, before_rest)
            before_wide = before_wide + wide[i]
            before_rest = before_rest + 1 - wide[i]
            there = first + rank
            layer_ref[there] = jnp.maximum(mats[i], 0) // 7
            kind_ref[there] = jnp.where(mats[i] >= 0, jnp.maximum(mats[i], 0) % 7, NONE)
            place_ref[there] = i

            @pl.when(mats[i] >= 0)
            def _():
                base_ref[mats[i]] = first
                rank_ref[mats[i]] = rank

        return jnp.maximum(level, count)

    level_ref[0] = lax.fori_loop(0, chips // GROUP, rank_group, jnp.int32(0))


def make_plan(owner, chips):
    matrices = owner.shape[0] * 7
    sizes = [chips, chips, chips, matrices, matrices, 1]
    smem = pl.BlockSpec(memory_space=pltpu.SMEM)
    return pl.pallas_call(
        plan_kernel,
        out_shape=[jax.ShapeDtypeStruct((size,), jnp.int32) for size in sizes],
        in_specs=[smem],
        out_specs=[smem] * len(sizes),
        scratch_shapes=[pltpu.SMEM((chips,), jnp.int32)],
        name="plan",
    )(owner)


def send_kernel(wide_ranks, layer_ref, kind_ref, grad_ref, out_ref):
    slot = pl.program_id(0)
    part = slot % GROUP
    group = slot - part
    rows = grad_ref.shape[1]
    lane = lax.broadcasted_iota(jnp.int32, (rows, LANES), 1)
    blank = jnp.zeros((rows, LANES), jnp.bfloat16)

    def tile_of(layer, at):
        return grad_ref[layer, :, pl.ds(pl.multiple_of(at * LANES, LANES), LANES)]

    for rank in range(GROUP):
        layer = layer_ref[group + rank]
        kind = kind_ref[group + rank]
        first = pick(kind, TILE0 + [0])
        offset = rank * WIDE if rank < wide_ranks else wide_ranks * (WIDE - 1) + rank
        is_wide = (kind >= FIRST_WIDE) & (kind < NONE)

        def put(at, value):
            out_ref[0, :, (offset + at) * LANES : (offset + at + 1) * LANES] = value

        def narrow():
            at = first + part
            low = pick(kind, STARTS + [0])
            high = low + pick(kind, WIDTHS + [0])
            column = lane + at * LANES
            keep = (column >= low) & (column < high)
            put(0, jnp.where(keep, tile_of(layer, at).astype(jnp.float32), 0.0).astype(jnp.bfloat16))

        if rank >= wide_ranks:
            narrow()
            continue

        @pl.when(is_wide)
        def _():
            for at in range(WIDE):
                tile = part * WIDE + at
                last = TILES[FIRST_WIDE] - 1
                if at < WIDE - (GROUP * WIDE - TILES[FIRST_WIDE]):
                    put(at, tile_of(layer, first + tile))
                else:
                    value = tile_of(layer, first + jnp.minimum(tile, last)).astype(jnp.float32)
                    put(at, (value * (tile <= last).astype(jnp.float32)).astype(jnp.bfloat16))

        @pl.when(jnp.logical_not(is_wide))
        def _():
            narrow()
            for at in range(1, WIDE):
                put(at, blank)


def build_send(wide_ranks, plan, grads):
    layers, rows, _ = grads.shape
    chips = plan[0].shape[0]
    cols = slot_tiles(wide_ranks) * LANES
    return pl.pallas_call(
        functools.partial(send_kernel, wide_ranks),
        out_shape=jax.ShapeDtypeStruct((chips, rows, cols), jnp.bfloat16),
        grid_spec=pltpu.PrefetchScalarGridSpec(
            num_scalar_prefetch=2,
            grid=(chips,),
            in_specs=[pl.BlockSpec((layers, rows, HALF), lambda i, *_: (0, 0, 0))],
            out_specs=pl.BlockSpec((1, rows, cols), lambda i, *_: (i, 0, 0)),
        ),
        name="build_send",
    )(plan[0], plan[1], grads)


def apply_kernel(wide_ranks, step_ref, core_ref, mine_ref, other_ref, grad_ref, out_ref, sum_ref):
    rank = pl.program_id(0)
    half = mine_ref.shape[1]
    core = core_ref[0]

    def run(tile, tiles):
        columns = pl.ds(pl.multiple_of(tile * LANES, LANES), tiles * LANES)
        block = grad_ref[:, columns]
        total = jnp.float32(0.0)
        for root_ref, side in ((mine_ref, core), (other_ref, 1 - core)):
            value = jnp.dot(root_ref[0], block, preferred_element_type=jnp.float32)
            value = value.astype(jnp.bfloat16)
            out_ref[pl.ds(pl.multiple_of(side * half, half), half), columns] = value
            wide_value = value.astype(jnp.float32)
            total = total + jnp.sum(wide_value * wide_value)
        sum_ref[rank] = total

    @pl.when(rank < wide_ranks)
    def _():
        run(rank * WIDE, WIDE)

    @pl.when(rank >= wide_ranks)
    def _():
        run(wide_ranks * (WIDE - 1) + rank, 1)


def apply_roots(wide_ranks, steps, core, mine, other, gathered):
    half, model_rows = mine.shape[1:]
    cols = gathered.shape[1]
    root_spec = pl.BlockSpec((1, half, model_rows), lambda r, steps, core: (steps[r], 0, 0))
    whole = pl.BlockSpec((model_rows, cols), lambda r, *_: (0, 0))
    return pl.pallas_call(
        functools.partial(apply_kernel, wide_ranks),
        out_shape=[
            jax.ShapeDtypeStruct((model_rows, cols), jnp.bfloat16),
            jax.ShapeDtypeStruct((GROUP,), jnp.float32),
        ],
        grid_spec=pltpu.PrefetchScalarGridSpec(
            num_scalar_prefetch=2,
            grid=(GROUP,),
            in_specs=[root_spec, root_spec, whole],
            out_specs=[whole, pl.BlockSpec(memory_space=pltpu.SMEM)],
        ),
        name="apply_roots",
    )(steps, core, mine, other, gathered)


def gram_kernel(wide_ranks, place_ref, core_ref, mine_ref, other_ref, out_ref):
    rank = pl.program_id(0)
    half = out_ref.shape[1]
    core = core_ref[0]

    def run(tile, tiles):
        columns = pl.ds(pl.multiple_of(tile * LANES, LANES), tiles * LANES)
        rows = pl.ds(pl.multiple_of(core * half, half), half)
        total = None
        for grad_ref in (mine_ref, other_ref):
            term = lax.dot_general(
                grad_ref[rows, columns],
                grad_ref[:, columns],
                (((1,), (1,)), ((), ())),
                preferred_element_type=jnp.float32,
            )
            total = term if total is None else total + term
        out_ref[0] = total.astype(jnp.bfloat16)

    @pl.when(rank < wide_ranks)
    def _():
        run(rank * WIDE, WIDE)

    @pl.when(rank >= wide_ranks)
    def _():
        run(wide_ranks * (WIDE - 1) + rank, 1)


def part_grams(wide_ranks, places, core, mine, other):
    model_rows, cols = mine.shape
    half = model_rows // 2
    whole = pl.BlockSpec((model_rows, cols), lambda r, *_: (0, 0))
    return pl.pallas_call(
        functools.partial(gram_kernel, wide_ranks),
        out_shape=jax.ShapeDtypeStruct((GROUP, half, model_rows), jnp.bfloat16),
        grid_spec=pltpu.PrefetchScalarGridSpec(
            num_scalar_prefetch=2,
            grid=(GROUP,),
            in_specs=[whole, whole],
            out_specs=pl.BlockSpec(
                (1, half, model_rows), lambda r, places, core: (places[r], 0, 0)
            ),
        ),
        name="part_grams",
    )(places, core, mine, other)


def update_kernel(wide_ranks, base_ref, rank_ref, scale_ref, weight_ref, back_ref, out_ref):
    layer = pl.program_id(0)
    rows = back_ref.shape[1]
    lane = lax.broadcasted_iota(jnp.int32, (rows, LANES), 1)
    for tile in range(ALL_TILES):
        step = None
        for kind in range(7):
            at = tile - TILE0[kind]
            if not 0 <= at < TILES[kind]:
                continue
            matrix = layer * 7 + kind
            rank = rank_ref[matrix]
            if kind >= FIRST_WIDE:
                source, column = at // WIDE, rank * WIDE + at % WIDE
            else:
                source, column = at, rank_tile(rank, wide_ranks)
            piece = back_ref[
                base_ref[matrix] + source, :, pl.ds(pl.multiple_of(column * LANES, LANES), LANES)
            ]
            piece = 0.02 * (scale_ref[matrix] * piece.astype(jnp.float32))
            low = STARTS[kind] - tile * LANES
            step = piece if step is None else jnp.where(lane >= low, piece, step)
        where = pl.ds(tile, rows, stride=ALL_TILES)
        out_ref[0, where, :] = weight_ref[0, where, :] - step


def update_weights(wide_ranks, plan, ratio, weights, returned):
    layers, rows = weights.shape[:2]
    view = (layers, rows * ALL_TILES, LANES)
    flat_spec = pl.BlockSpec((1,) + view[1:], lambda l, *_: (l, 0, 0))
    out = pl.pallas_call(
        functools.partial(update_kernel, wide_ranks),
        out_shape=jax.ShapeDtypeStruct(view, jnp.float32),
        grid_spec=pltpu.PrefetchScalarGridSpec(
            num_scalar_prefetch=3,
            grid=(layers,),
            in_specs=[flat_spec, pl.BlockSpec(returned.shape, lambda l, *_: (0, 0, 0))],
            out_specs=flat_spec,
        ),
        name="update_weights",
    )(plan[3], plan[4], ratio.reshape(-1), weights.reshape(view), returned)
    return out.reshape(weights.shape)


def kind_sums(values):
    return jnp.stack(
        [
            jnp.sum(values[:, :, start : start + wide], axis=(1, 2))
            for start, wide in zip(STARTS, WIDTHS)
        ],
        axis=1,
    )


def swap_cores(value):
    return lax.ppermute(value, "tp", [(0, 1), (1, 0)])


def swap_chips(value, step):
    chips = lax.axis_size("fsdp")
    return lax.ppermute(value, "fsdp", [(i, i ^ step) for i in range(chips)])


def sum_everywhere(value):
    value = value + swap_cores(value)
    step = 1
    while step < lax.axis_size("fsdp"):
        value = value + swap_chips(value, step)
        step = 2 * step
    return value


def refresh(
    wide_ranks, plan, grads, weights, adam_m, adam_v, stats, roots, vec_weight, vec_grad, vec_m, vec_v
):
    chips = lax.axis_size("fsdp")
    chip = lax.axis_index("fsdp")
    core = lax.axis_index("tp").astype(jnp.int32)
    layers = grads.shape[0]
    rows = grads.shape[1]
    model_rows = rows * chips
    cols = slot_tiles(wide_ranks) * LANES
    group_first = chip - chip % GROUP
    kinds = lax.dynamic_slice(plan[1], (group_first,), (GROUP,))
    places = lax.dynamic_slice(plan[2], (group_first,), (GROUP,))
    own_part = (chip % GROUP).astype(jnp.int32)
    owned = jnp.any((places == own_part) & (kinds < NONE))
    core_arg = core.reshape(1)

    outgoing = build_send(wide_ranks, plan, grads[:, :, 0, :])
    arrived = lax.all_to_all(outgoing, "fsdp", split_axis=0, concat_axis=0, tiled=True)
    gathered = arrived.reshape(model_rows, cols)

    root_mine = jnp.stack([roots[0]] + [swap_chips(roots[0], step) for step in range(1, GROUP)])
    root_other = swap_cores(root_mine)

    grad_float = grads.astype(jnp.float32)
    adam_m_new = 0.9 * adam_m + 0.1 * grad_float
    adam_v_new = 0.99 * adam_v + 0.01 * grad_float * grad_float
    adam_step = (adam_m_new / (jnp.sqrt(adam_v_new) + 1e-08))[:, :, 0, :]
    adam_part = kind_sums(adam_step * adam_step)

    precond, sums = apply_roots(
        wide_ranks, places ^ own_part, core_arg, root_mine, root_other, gathered
    )
    returned = lax.all_to_all(
        precond.reshape(chips, rows, cols), "fsdp", split_axis=0, concat_axis=0, tiled=True
    )
    ranks = jnp.arange(GROUP, dtype=jnp.int32)
    is_here = (plan[3] == group_first)[:, None] & (plan[4][:, None] == ranks[None, :])
    shampoo_part = jnp.sum(jnp.where(is_here, sums[None, :], 0.0), axis=1).reshape(layers, 7)
    totals = sum_everywhere(jnp.stack([adam_part, shampoo_part]))
    ratio = jnp.sqrt(totals[0]) / (jnp.sqrt(totals[1]) + 1e-06)

    grams = part_grams(wide_ranks, places, core_arg, gathered, swap_cores(gathered))
    groups = [[first + i for i in range(GROUP)] for first in range(0, chips, GROUP)]
    terms = lax.all_to_all(
        grams, "fsdp", split_axis=0, concat_axis=0, tiled=True, axis_index_groups=groups
    )
    stat_term = jnp.sum(terms.astype(jnp.float32), axis=0)
    stats_new = jnp.where(owned, 0.9 * stats[0] + 0.1 * stat_term, stats[0])[None]

    weights_new = update_weights(wide_ranks, plan, ratio, weights, returned)

    vec_float = vec_grad.astype(jnp.float32)
    vec_m_new = 0.9 * vec_m + 0.1 * vec_float
    vec_v_new = 0.99 * vec_v + 0.01 * vec_float * vec_float
    vec_weight_new = vec_weight - 0.02 * vec_m_new / (jnp.sqrt(vec_v_new) + 1e-08)
    return (weights_new, adam_m_new, adam_v_new, stats_new, vec_weight_new, vec_m_new, vec_v_new)


def on_device(owner, *arrays):
    plan = make_plan(owner, lax.axis_size("fsdp"))
    branches = [functools.partial(refresh, wide_ranks) for wide_ranks in range(2, GROUP + 1)]
    return lax.switch(plan[5][0] - 2, branches, plan, *arrays)


def solution(mesh):
    matrix = P(None, "fsdp", "tp", None)
    slot = P("fsdp", "tp", None)
    vector = P(None, ("fsdp", "tp"))
    return jax.shard_map(
        on_device,
        mesh=mesh,
        in_specs=(P(), matrix, matrix, matrix, matrix, slot, slot, vector, vector, vector, vector),
        out_specs=(matrix, matrix, matrix, slot, vector, vector, vector),
        check_vma=False,
    )
```

time: 272 us -> 253 us (0.930)
  matrix products: 19.1 us -> 0 us
  Pallas kernels: 18.9 us -> 34.8 us
  other arithmetic: 31.3 us -> 16.7 us
  starting transfers between devices: 29.3 us -> 21 us
  waiting for transfers between devices: 82.6 us -> 88.5 us
  local copies, waits for them, and re-layouts: 12.6 us -> 18 us
  blocking collectives: 76.4 us -> 72.1 us
    psum x1 -> x0, blocking collectives: 76.4 us -> none  [on_device(): adam_total, shampoo_total = lax.psum((adam_part, mine), ('fsdp', 'tp'))]
    all_to_all x0 -> x1, blocking collectives: none -> 72.1 us  [refresh(): lax.all_to_all(outgoing, 'fsdp', split_axis=0, concat_axis=0, tiled=True)]
    ppermute x0 -> x7, waiting for transfers between devices: none -> 60.1 us  [swap_chips(): return lax.ppermute(value, 'fsdp', [(i, i ^ step) for i in range(chips)])]
    all_to_all x2, waiting for transfers between devices: 80.4 us -> 27.2 us  [the longest x1 27.2 us: refresh(): lax.all_to_all(grams, 'fsdp', split_axis=0, concat_axis=0, tiled=True, ax...]
    all_to_all x2, starting transfers between devices: 29.2 us -> 9.3 us  [the longest x1 4.67 us: refresh(): lax.all_to_all(grams, 'fsdp', split_axis=0, concat_axis=0, tiled=True, ax...]
    dot_general x2 -> x0, matrix products: 19.1 us -> none  [the longest x1 10.5 us: on_device(): jnp.dot(root, gathered, preferred_element_type=jnp.float32)]
    pallas_call x2 -> x5, Pallas kernels: 18.9 us -> 34.8 us  [the longest x1 10.6 us: apply_roots(): pl.pallas_call(functools.partial(apply_kernel, wide_ranks), out_shape=[ja...]
    cond x0 -> x26, local copies, waits for them, and re-layouts: none -> 15.4 us  [the longest x2 13.6 us: on_device(): return lax.switch(plan[5][0] - 2, branches, plan, *arrays)]
  transfers between devices with their start and end apart: 4 -> 12, of which waited for: 2 -> 8; matrix products, arithmetic and copies ran while one was open for 16% -> 13% of each run, Pallas kernels for 0% -> 8%
where the time goes in v2:
time: 253 us
  waiting for transfers between devices  88.5 us (35%)
  blocking collectives  72.1 us (28%)
  Pallas kernels  34.8 us (14%)
  starting transfers between devices  21 us (8%)
  local copies, waits for them, and re-layouts  18 us (7%)
  other arithmetic  16.7 us (7%)
    all_to_all x1, blocking collectives, refresh(): lax.all_to_all(outgoing, 'fsdp', split_axis=0, concat_axis=0, tiled=True)  72.1 us
    ppermute x7, waiting for transfers between devices, swap_chips(): return lax.ppermute(value, 'fsdp', [(i, i ^ step) for i in range(chips)])  60.1 us
    all_to_all x1, waiting for transfers between devices, refresh(): lax.all_to_all(grams, 'fsdp', split_axis=0, concat_axis=0, tiled=True, ax...  27.2 us
    cond x2, local copies, waits for them, and re-layouts, on_device(): return lax.switch(plan[5][0] - 2, branches, plan, *arrays)  13.6 us
    ppermute x7, starting transfers between devices, swap_chips(): return lax.ppermute(value, 'fsdp', [(i, i ^ step) for i in range(chips)])  11.7 us
    pallas_call x1, Pallas kernels, apply_roots(): pl.pallas_call(functools.partial(apply_kernel, wide_ranks), out_shape=[ja...  10.6 us
    pallas_call x1, Pallas kernels, part_grams(): pl.pallas_call(functools.partial(gram_kernel, wide_ranks), out_shape=jax....  8.82 us
    pallas_call x1, Pallas kernels, build_send(): pl.pallas_call(functools.partial(send_kernel, wide_ranks), out_shape=jax....  8.22 us
  transfers between devices with their start and end apart: 12, of which 8 were waited for; matrix products, arithmetic and copies ran while one was open for 13% of the time, Pallas kernels for 8%

profile of v2, /device:TPU:0, one launch (start us, length us, event | category | flops | bytes accessed | tf_op | source)
XLA Modules:
  0.0 252.6 jit_solution(15636409599153175008)
XLA Ops:
  0.6 1.9 plan.1
  3.2 248.2 %conditional.1 = (f32[1,448,896]{2,1,0:T(8,128)S(1)}, f32[2,92]{1,0:T(2,128)S(1)}, f32[2,92]{1,0:T(2,128)S(1)}, f32[2,92]{1,0:T(2,128)S(1)}, f32[2,56,1,8320]{3,...) conditional(s32[]{:T(128)} %bitcast.63, ...), branch_computations={%region_0.11_spmd, %region_11.22_spmd, %region_22.33_spmd} | conditional | flops 20417202 | bytes 194790496 | solution.py:393
  3.2 8.2 %build_send.3 = bf16[16,56,1536]{2,1,0:T(8,128)(2,1)} custom-call(s32[16]{0:T(128)S(1)} %get-tuple-element.97.layer_ref, s32[16]{0:T(128)S(1)} %get-tuple-element.98.kind_ref, bf16[2,56,8320]{2,1,0:T(8,128)(2,1)} %bitcast.88), custom_call_target="tpu_custom_call" | custom-call | tf_op jit(solution)/shard_map/cond/branch_0_fun/build_send/pallas_call | solution.py:152
  11.5 72.1 %all_to_all.36 = bf16[16,56,1536]{2,1,0:T(8,128)(2,1)S(1)} all-to-all(bf16[16,56,1536]{2,1,0:T(8,128)(2,1)} %build_send.3), channel_id=1, replica_groups=mesh['fsdp'=16,'tp'=2] {'fsdp'}, dimensions={0} | all-to-all | bytes 5505024 | tf_op jit(solution)/shard_map/cond/branch_0_fun/all_to_all | solution.py:349
  84.3 1.4 collective-permute-start.1
  85.7 1.5 collective-permute-start
  87.1 18.2 %collective-permute-done.2 = bf16[448,896]{1,0:T(8,128)(2,1)S(1)} collective-permute-done((bf16[448,896]{1,0:T(8,128)(2,1)S(1)}, bf16[448,896]{1,0:T(8,128)(2,1)S(1)}, u32[]{:S(2)}, u32[]{:S(2)}) %collective-permute-start.2) | collective-permute-done | bytes 802848 | tf_op jit(solution)/shard_map/cond/branch_0_fun/ppermute | solution.py:319
  105.3 16.2 %collective-permute-done.1 = bf16[448,896]{1,0:T(8,128)(2,1)S(1)} collective-permute-done((bf16[448,896]{1,0:T(8,128)(2,1)S(1)}, bf16[448,896]{1,0:T(8,128)(2,1)S(1)}, u32[]{:S(2)}, u32[]{:S(2)}) %collective-permute-start.1) | collective-permute-done | bytes 802848 | tf_op jit(solution)/shard_map/cond/branch_0_fun/ppermute | solution.py:319
  121.5 1.9 pad_maximum_fusion.mine_ref
  124.0 8.8 %part_grams.3 = bf16[4,448,896]{2,1,0:T(8,128)(2,1)} custom-call(s32[4]{0:T(128)} %get-tuple-element.351.place_ref, s32[1]{0:T(128)} %bitcast.core_ref, bf16[896,1536]{1,0:T(8,128)(2,1)} %bitcast.95, bf16[896,1536]{1,0:T(8,128)(2,1)} %collective-permute-done.9.other_ref), custom_call_target="tpu_custom_call" | custom-call | tf_op jit(solution)/shard_map/cond/branch_0_fun/part_grams/pallas_call | solution.py:244
  132.8 4.7 %all-to-all-start.2 = ((bf16[4,448,896]{2,1,0:T(8,128)(2,1)}), bf16[4,448,896]{2,1,0:T(8,128)(2,1)}, u32[]{:S(2)}, u32[]{:S(2)}) async-start(bf16[4,448,896]{2,1,0:T(8,128)(2,1)} %part_grams.3), calls=%async_computation.2 | async-start | bytes 6422528 | tf_op jit(solution)/shard_map/cond/branch_0_fun/all_to_all | solution.py:375
  137.5 10.6 %apply_roots.3 = (bf16[896,1536]{1,0:T(8,128)(2,1)}, f32[4]{0:T(128)}) custom-call(s32[4]{0:T(128)} %get-tuple-element.350.step_ref, s32[1]{0:T(128)} %bitcast.core_ref, bf16[4,448,896]{2,1,0:T(8,128)(2,1)} %pad_maximum_fusion.mine_ref, bf16[4,448,896]{2,1,0:T(8,128)(2,1)} %collective-permute-done.3.other_ref, bf16[896,1536]{1,0:T(8,128)(2,1)} %bitcast.96), custom_call_target="tpu_custom_call" | custom-call | tf_op jit(solution)/shard_map/cond/branch_0_fun/apply_roots/pallas_call | solution.py:196
  148.1 27.2 %all-to-all-done.2 = bf16[4,448,896]{2,1,0:T(8,128)(2,1)} async-done(((bf16[4,448,896]{2,1,0:T(8,128)(2,1)}), bf16[4,448,896]{2,1,0:T(8,128)(2,1)}, u32[]{:S(2)}, u32[]{:S(2)}) %all-to-all-start.2) | async-done | bytes 3211296 | tf_op jit(solution)/shard_map/cond/branch_0_fun/all_to_all | solution.py:375
  175.3 4.6 %all-to-all-start.1 = ((bf16[16,56,1536]{2,1,0:T(8,128)(2,1)}), bf16[16,56,1536]{2,1,0:T(8,128)(2,1)}, u32[]{:S(2)}, u32[]{:S(2)}) async-start(bf16[16,56,1536]{2,1,0:T(8,128)(2,1)} %bitcast.111), calls=%async_computation.1 | async-start | bytes 5505024 | tf_op jit(solution)/shard_map/cond/branch_0_fun/all_to_all | solution.py:364
  180.0 6.3 %multiply_bitcast_fusion = (f32[2,56,8320]{2,1,0:T(8,128)S(1)}, f32[2,56,1,8320]{3,1,0,2:T(8,128)}, f32[2,56,1,8320]{3,1,0,2:T(8,128)}) fusion(bf16[2,56,1,8320]{3,1,2,0:T(8,128)(2,1)S(1)} %copy-done, f32[2,56,1,8320]{3,2,1,0:T(1,128)} %get-tuple-element.273, f32[2,56,1,8320]{3,2,1,0:T(1,128)} %get-tuple-element.271), kind=kLoop, calls=%fused_computation.7 | loop fusion | flops 10250240 | bytes 20500480 | tf_op jit(solution)/shard_map/cond/branch_0_fun/mul | solution.py:359
  186.3 1.8 copy-done.4
  188.5 1.2 slice_reduce_fusion.3
  189.9 2.2 slice_reduce_fusion
  192.7 1.2 collective-permute-done.4
  193.9 1.6 collective-permute-start.5
  195.5 2.0 collective-permute-done.5
  197.5 1.6 collective-permute-start.6
  199.8 1.3 collective-permute-done.6
  201.1 1.6 collective-permute-start.7
  202.7 7.9 %copy.135 = f32[2,56,1,8320]{3,2,1,0:T(1,128)} copy(f32[2,56,1,8320]{3,1,0,2:T(8,128)} %get-tuple-element.348) | data formatting | bytes 7454720 | tf_op jit(solution)/shard_map/cond | solution.py:393
  210.6 14.9 %collective-permute-done.7 = f32[2,2,7]{2,1,0:T(2,128)S(1)} collective-permute-done((f32[2,2,7]{2,1,0:T(2,128)S(1)}, f32[2,2,7]{2,1,0:T(2,128)S(1)}, u32[]{:S(2)}, u32[]{:S(2)}) %collective-permute-start.7) | collective-permute-done | bytes 144 | tf_op jit(solution)/shard_map/cond/branch_0_fun/ppermute | solution.py:319
  225.5 3.4 %collective-permute-start.8 = (f32[2,2,7]{2,1,0:T(2,128)S(1)}, f32[2,2,7]{2,1,0:T(2,128)S(1)}, u32[]{:S(2)}, u32[]{:S(2)}) collective-permute-start(f32[2,2,7]{2,1,0:T(2,128)S(1)} %add.116), channel_id=1, source_target_pairs={{0,16},{2,18},{4,20},{6,22},{8,24},{10,26},{12,28},{14,30},{16,0},... | collective-permute-start | bytes 344 | tf_op jit(solution)/shard_map/cond/branch_0_fun/ppermute | solution.py:319
  228.9 5.7 %copy.132 = f32[2,56,1,8320]{3,2,1,0:T(1,128)} copy(f32[2,56,1,8320]{3,1,0,2:T(8,128)S(1)} %copy-done.7) | data formatting | bytes 7454720 | tf_op jit(solution)/shard_map/cond | solution.py:393
  234.6 7.6 %collective-permute-done.8 = f32[2,2,7]{2,1,0:T(2,128)S(1)} collective-permute-done((f32[2,2,7]{2,1,0:T(2,128)S(1)}, f32[2,2,7]{2,1,0:T(2,128)S(1)}, u32[]{:S(2)}, u32[]{:S(2)}) %collective-permute-start.8) | collective-permute-done | bytes 144 | tf_op jit(solution)/shard_map/cond/branch_0_fun/ppermute | solution.py:319
  242.8 2.5 convert_reduce_fusion
  246.2 5.2 %update_weights.3 = f32[2,3640,128]{2,1,0:T(8,128)} custom-call(s32[14]{0:T(128)S(1)} %get-tuple-element.90.base_ref, s32[14]{0:T(128)S(1)} %get-tuple-element.91.rank_ref, f32[14]{0:T(128)} %div.29.scale_ref, f32[2,3640,128]{2,1,0:T(8,128)} %bitcast.91, bf16[16,56,1536]{2,1,0:T(8,128)(2,1)} %all-to-all-done.1.back_ref), custom_call_target="tpu_custom_call" | custom-call | tf_op jit(solution)/shard_map/cond/branch_0_fun/update_weights/pallas_call | solution.py:289
  251.5 1.1 copy-done.19
  (62 shorter events, 4.7 us)
Async XLA Ops:
  11.5 72.1 %copy-start.15 = (bf16[1,448,896]{2,1,0:T(8,128)(2,1)S(1)}, bf16[1,448,896]{2,1,0:T(8,128)(2,1)}, u32[]{:S(2)}) copy-start(bf16[1,448,896]{2,1,0:T(8,128)(2,1)} %get-tuple-element.96) | copy-start | bytes 2408452 | tf_op jit(solution)/shard_map/cond
  83.6 40.4 %copy-start.3 = (bf16[16,56,1536]{2,1,0:T(8,128)(2,1)}, bf16[16,56,1536]{2,1,0:T(8,128)(2,1)S(1)}, u32[]{:S(2)}) copy-start(bf16[16,56,1536]{2,1,0:T(8,128)(2,1)S(1)} %all_to_all.36) | copy-start | bytes 8257540 | tf_op jit(solution)/shard_map/cond
  83.6 40.4 %collective-permute-start.9 = (bf16[896,1536]{1,0:T(8,128)(2,1)S(1)}, bf16[896,1536]{1,0:T(8,128)(2,1)}, u32[]{:S(2)}, u32[]{:S(2)}) collective-permute-start(bf16[896,1536]{1,0:T(8,128)(2,1)S(1)} %bitcast.94), channel_id=1, source_target_pairs={{0,1},{1,0},{2,3},{3,2},{4,5},{5,4},{6,7},{7,6},{8,9},{9,8},{10,11... | collective-permute-start | bytes 8257544 | tf_op jit(solution)/shard_map/cond/branch_0_fun/ppermute | solution.py:314
  83.6 21.7 %collective-permute-start.2 = (bf16[448,896]{1,0:T(8,128)(2,1)S(1)}, bf16[448,896]{1,0:T(8,128)(2,1)S(1)}, u32[]{:S(2)}, u32[]{:S(2)}) collective-permute-start(bf16[448,896]{1,0:T(8,128)(2,1)S(1)} %bitcast.97), channel_id=1, source_target_pairs={{0,6},{2,4},{4,2},{6,0},{8,14},{10,12},{12,10},{14,8},{16,22},{18,... | collective-permute-start | bytes 2408456 | tf_op jit(solution)/shard_map/cond/branch_0_fun/ppermute | solution.py:319
  84.3 37.2 %collective-permute-start.1 = (bf16[448,896]{1,0:T(8,128)(2,1)S(1)}, bf16[448,896]{1,0:T(8,128)(2,1)S(1)}, u32[]{:S(2)}, u32[]{:S(2)}) collective-permute-start(bf16[448,896]{1,0:T(8,128)(2,1)S(1)} %bitcast.98), channel_id=1, source_target_pairs={{0,4},{2,6},{4,0},{6,2},{8,12},{10,14},{12,8},{14,10},{16,20},{18,... | collective-permute-start | bytes 2408456 | tf_op jit(solution)/shard_map/cond/branch_0_fun/ppermute | solution.py:319
  85.7 35.8 %collective-permute-start = (bf16[448,896]{1,0:T(8,128)(2,1)S(1)}, bf16[448,896]{1,0:T(8,128)(2,1)S(1)}, u32[]{:S(2)}, u32[]{:S(2)}) collective-permute-start(bf16[448,896]{1,0:T(8,128)(2,1)S(1)} %bitcast.99), channel_id=1, source_target_pairs={{0,2},{2,0},{4,6},{6,4},{8,10},{10,8},{12,14},{14,12},{16,18},{18,... | collective-permute-start | bytes 2408456 | tf_op jit(solution)/shard_map/cond/branch_0_fun/ppermute | solution.py:319
  123.4 14.1 %collective-permute-start.3 = (bf16[4,448,896]{2,1,0:T(8,128)(2,1)}, bf16[4,448,896]{2,1,0:T(8,128)(2,1)}, u32[]{:S(2)}, u32[]{:S(2)}) collective-permute-start(bf16[4,448,896]{2,1,0:T(8,128)(2,1)} %pad_maximum_fusion.mine_ref), channel_id=1, source_target_pairs={{0,1},{1,0},{2,3},{3,2},{4,5},{5,4},{6,7},{7,6},{8,9},{9,8},{10,11... | collective-permute-start | bytes 9633800 | tf_op jit(solution)/shard_map/cond/branch_0_fun/ppermute | solution.py:314
  132.8 42.5 %all-to-all-start.2 = ((bf16[4,448,896]{2,1,0:T(8,128)(2,1)}), bf16[4,448,896]{2,1,0:T(8,128)(2,1)}, u32[]{:S(2)}, u32[]{:S(2)}) async-start(bf16[4,448,896]{2,1,0:T(8,128)(2,1)} %part_grams.3), calls=%async_computation.2 | async-start | bytes 6422528 | tf_op jit(solution)/shard_map/cond/branch_0_fun/all_to_all | solution.py:375
  148.1 31.9 %copy-start = (bf16[2,56,1,8320]{3,1,2,0:T(8,128)(2,1)S(1)}, bf16[2,56,1,8320]{3,1,2,0:T(8,128)(2,1)}, u32[]{:S(2)}) copy-start(bf16[2,56,1,8320]{3,1,2,0:T(8,128)(2,1)} %get-tuple-element.272) | copy-start | bytes 5591044 | tf_op jit(solution)/shard_map/cond
  175.3 70.9 %all-to-all-start.1 = ((bf16[16,56,1536]{2,1,0:T(8,128)(2,1)}), bf16[16,56,1536]{2,1,0:T(8,128)(2,1)}, u32[]{:S(2)}, u32[]{:S(2)}) async-start(bf16[16,56,1536]{2,1,0:T(8,128)(2,1)} %bitcast.111), calls=%async_computation.1 | async-start | bytes 5505024 | tf_op jit(solution)/shard_map/cond/branch_0_fun/all_to_all | solution.py:364
  186.3 1.9 copy-start.4
  186.3 6.3 %copy-start.38 = (f32[4]{0:T(128)S(1)}, f32[4]{0:T(128)}, u32[]{:S(2)}) copy-start(f32[4]{0:T(128)} %get-tuple-element.99) | copy-start | bytes 52 | tf_op jit(solution)/shard_map/cond
  186.3 9.2 %copy-start.20 = (f32[2,92]{1,0:T(2,128)S(1)}, f32[2,92]{1,0:T(2,128)}, u32[]{:S(2)}) copy-start(f32[2,92]{1,0:T(2,128)} %get-tuple-element.104) | copy-start | bytes 2212 | tf_op jit(solution)/shard_map/cond
  186.3 9.2 %copy-start.23 = (f32[2,92]{1,0:T(2,128)S(1)}, f32[2,92]{1,0:T(2,128)}, u32[]{:S(2)}) copy-start(f32[2,92]{1,0:T(2,128)} %get-tuple-element.106) | copy-start | bytes 2212 | tf_op jit(solution)/shard_map/cond
  186.3 9.2 %copy-start.26 = (f32[2,92]{1,0:T(2,128)S(1)}, f32[2,92]{1,0:T(2,128)}, u32[]{:S(2)}) copy-start(f32[2,92]{1,0:T(2,128)} %get-tuple-element.103) | copy-start | bytes 2212 | tf_op jit(solution)/shard_map/cond
  186.3 9.2 %copy-start.32 = (bf16[2,92]{1,0:T(2,128)(2,1)S(1)}, bf16[2,92]{1,0:T(2,128)(2,1)}, u32[]{:S(2)}) copy-start(bf16[2,92]{1,0:T(2,128)(2,1)} %get-tuple-element.105) | copy-start | bytes 1108 | tf_op jit(solution)/shard_map/cond
  186.3 12.7 %copy-start.29 = (s32[4]{0:T(128)S(1)}, s32[4]{0:T(128)}, u32[]{:S(2)}) copy-start(s32[4]{0:T(128)} %get-tuple-element.351.place_ref) | copy-start | bytes 52 | tf_op jit(solution)/shard_map/cond
  192.7 1.2 collective-permute-start.4
  193.9 3.6 %collective-permute-start.5 = (f32[2,2,7]{2,1,0:T(2,128)S(1)}, f32[2,2,7]{2,1,0:T(2,128)S(1)}, u32[]{:S(2)}, u32[]{:S(2)}) collective-permute-start(f32[2,2,7]{2,1,0:T(2,128)S(1)} %fusion.8), channel_id=1, source_target_pairs={{0,2},{2,0},{4,6},{6,4},{8,10},{10,8},{12,14},{14,12},{16,18},{18,... | collective-permute-start | bytes 344 | tf_op jit(solution)/shard_map/cond/branch_0_fun/ppermute | solution.py:319
  197.5 3.6 %collective-permute-start.6 = (f32[2,2,7]{2,1,0:T(2,128)S(1)}, f32[2,2,7]{2,1,0:T(2,128)S(1)}, u32[]{:S(2)}, u32[]{:S(2)}) collective-permute-start(f32[2,2,7]{2,1,0:T(2,128)S(1)} %fusion.39), channel_id=1, source_target_pairs={{0,4},{2,6},{4,0},{6,2},{8,12},{10,14},{12,8},{14,10},{16,20},{18,... | collective-permute-start | bytes 344 | tf_op jit(solution)/shard_map/cond/branch_0_fun/ppermute | solution.py:319
  201.1 24.4 %collective-permute-start.7 = (f32[2,2,7]{2,1,0:T(2,128)S(1)}, f32[2,2,7]{2,1,0:T(2,128)S(1)}, u32[]{:S(2)}, u32[]{:S(2)}) collective-permute-start(f32[2,2,7]{2,1,0:T(2,128)S(1)} %add.115), channel_id=1, source_target_pairs={{0,8},{2,10},{4,12},{6,14},{8,0},{10,2},{12,4},{14,6},{16,24},{18,... | collective-permute-start | bytes 344 | tf_op jit(solution)/shard_map/cond/branch_0_fun/ppermute | solution.py:319
  202.7 26.2 %copy-start.7 = (f32[2,56,1,8320]{3,1,0,2:T(8,128)S(1)}, f32[2,56,1,8320]{3,1,0,2:T(8,128)}, u32[]{:S(2)}) copy-start(f32[2,56,1,8320]{3,1,0,2:T(8,128)} %get-tuple-element.349) | copy-start | bytes 11182084 | tf_op jit(solution)/shard_map/cond
  225.5 16.6 %collective-permute-start.8 = (f32[2,2,7]{2,1,0:T(2,128)S(1)}, f32[2,2,7]{2,1,0:T(2,128)S(1)}, u32[]{:S(2)}, u32[]{:S(2)}) collective-permute-start(f32[2,2,7]{2,1,0:T(2,128)S(1)} %add.116), channel_id=1, source_target_pairs={{0,16},{2,18},{4,20},{6,22},{8,24},{10,26},{12,28},{14,30},{16,0},... | collective-permute-start | bytes 344 | tf_op jit(solution)/shard_map/cond/branch_0_fun/ppermute | solution.py:319
  234.6 10.7 %copy-start.10 = (f32[1,448,896]{2,1,0:T(8,128)S(1)}, f32[1,448,896]{2,1,0:T(8,128)}, u32[]{:S(2)}) copy-start(f32[1,448,896]{2,1,0:T(8,128)} %get-tuple-element.102) | copy-start | bytes 4816900 | tf_op jit(solution)/shard_map/cond
  251.5 1.2 copy-start.19
  251.5 1.2 copy-start.35
  251.5 1.2 copy-start.36
  251.5 1.1 copy-start.37

commit v3 on v2

v3 whole, which is shorter than its diff:
```python
import functools

import jax
import jax.numpy as jnp
from jax import lax
from jax.experimental import pallas as pl
from jax.experimental.pallas import tpu as pltpu
from jax.sharding import PartitionSpec as P

FF = 4864
QW = 896
KW = 128
LANES = 128
WIDTHS = [QW // 2, KW // 2, KW // 2, QW // 2, FF // 2, FF // 2, FF // 2]
STARTS = [sum(WIDTHS[:kind]) for kind in range(7)]
TILE0 = [start // LANES for start in STARTS]
TILES = [-(-(start + wide) // LANES) - start // LANES for start, wide in zip(STARTS, WIDTHS)]
HALF = sum(WIDTHS)
ALL_TILES = HALF // LANES
GROUP = 4
WIDE = -(-max(TILES) // GROUP)
FIRST_WIDE = 4
NONE = 7


def pick(index, values):
    result = jnp.int32(values[-1])
    for at in range(len(values) - 1):
        result = jnp.where(index == at, values[at], result)
    return result


def row_block(rows):
    return 8 if rows % 8 == 0 else rows


def rank_tile(rank, wide_ranks):
    return jnp.where(rank < wide_ranks, rank * WIDE, wide_ranks * (WIDE - 1) + rank)


def slot_tiles(wide_ranks):
    return wide_ranks * WIDE + GROUP - wide_ranks


def plan_kernel(owner_ref, layer_ref, kind_ref, place_ref, base_ref, rank_ref, level_ref, mat_ref):
    layers = owner_ref.shape[0]
    chips = layer_ref.shape[0]

    def clear(chip, carry):
        mat_ref[chip] = -1
        return carry

    lax.fori_loop(0, chips, clear, 0)

    def name(matrix, carry):
        mat_ref[owner_ref[matrix // 7, matrix % 7]] = matrix
        return carry

    lax.fori_loop(0, layers * 7, name, 0)

    def rank_group(group, level):
        first = group * GROUP
        mats = [mat_ref[first + i] for i in range(GROUP)]
        wide = [((m >= 0) & (m % 7 >= FIRST_WIDE)).astype(jnp.int32) for m in mats]
        count = sum(wide)
        before_wide = jnp.int32(0)
        before_rest = count
        for i in range(GROUP):
            rank = jnp.where(wide[i] == 1, before_wide, before_rest)
            before_wide = before_wide + wide[i]
            before_rest = before_rest + 1 - wide[i]
            there = first + rank
            layer_ref[there] = jnp.maximum(mats[i], 0) // 7
            kind_ref[there] = jnp.where(mats[i] >= 0, jnp.maximum(mats[i], 0) % 7, NONE)
            place_ref[there] = i

            @pl.when(mats[i] >= 0)
            def _():
                base_ref[mats[i]] = first
                rank_ref[mats[i]] = rank

        return jnp.maximum(level, count)

    level_ref[0] = lax.fori_loop(0, chips // GROUP, rank_group, jnp.int32(0))


def make_plan(owner, chips):
    matrices = owner.shape[0] * 7
    sizes = [chips, chips, chips, matrices, matrices, 1]
    smem = pl.BlockSpec(memory_space=pltpu.SMEM)
    return pl.pallas_call(
        plan_kernel,
        out_shape=[jax.ShapeDtypeStruct((size,), jnp.int32) for size in sizes],
        in_specs=[smem],
        out_specs=[smem] * len(sizes),
        scratch_shapes=[pltpu.SMEM((chips,), jnp.int32)],
        name="plan",
    )(owner)


def send_kernel(wide_ranks, layer_ref, kind_ref, grad_ref, out_ref):
    group = pl.program_id(0) * GROUP
    rows = grad_ref.shape[1]
    lane = lax.broadcasted_iota(jnp.int32, (rows, LANES), 1)
    last = max(TILES) - 1

    def tile_of(layer, at):
        return grad_ref[layer, :, pl.ds(pl.multiple_of(at * LANES, LANES), LANES)]

    def fill(part, carry):
        for rank in range(GROUP):
            layer = layer_ref[group + rank]
            kind = kind_ref[group + rank]
            first = pick(kind, TILE0 + [0])
            offset = rank * WIDE if rank < wide_ranks else wide_ranks * (WIDE - 1) + rank

            def put(at, value):
                out_ref[part, :, (offset + at) * LANES : (offset + at + 1) * LANES] = value

            def narrow():
                at = first + part
                low = pick(kind, STARTS + [0])
                high = low + pick(kind, WIDTHS + [0])
                column = lane + at * LANES
                value = jnp.where(
                    (column >= low) & (column < high), tile_of(layer, at).astype(jnp.float32), 0.0
                )
                put(0, value.astype(jnp.bfloat16))

            if rank >= wide_ranks:
                narrow()
                continue

            is_wide = (kind >= FIRST_WIDE) & (kind < NONE)

            @pl.when(is_wide)
            def _():
                for at in range(WIDE):
                    tile = part * WIDE + at
                    value = tile_of(layer, first + jnp.minimum(tile, last))
                    if (GROUP - 1) * WIDE + at > last:
                        value = value.astype(jnp.float32) * (tile <= last).astype(jnp.float32)
                    put(at, value.astype(jnp.bfloat16))

            @pl.when(jnp.logical_not(is_wide))
            def _():
                narrow()
                for at in range(1, WIDE):
                    put(at, jnp.zeros((rows, LANES), jnp.bfloat16))

        return carry

    lax.fori_loop(0, GROUP, fill, 0)


def build_send(wide_ranks, plan, grads):
    layers, rows, _ = grads.shape
    chips = plan[0].shape[0]
    cols = slot_tiles(wide_ranks) * LANES
    return pl.pallas_call(
        functools.partial(send_kernel, wide_ranks),
        out_shape=jax.ShapeDtypeStruct((chips, rows, cols), jnp.bfloat16),
        grid_spec=pltpu.PrefetchScalarGridSpec(
            num_scalar_prefetch=2,
            grid=(chips // GROUP,),
            in_specs=[pl.BlockSpec((layers, rows, HALF), lambda g, *_: (0, 0, 0))],
            out_specs=pl.BlockSpec((GROUP, rows, cols), lambda g, *_: (g, 0, 0)),
        ),
        name="build_send",
    )(plan[0], plan[1], grads)


def adam_kernel(grad_ref, m_ref, v_ref, m_out, v_out, sum_ref, grad_flat, total_ref):
    layer = pl.program_id(0)
    block = grad_ref.shape[1]
    for tile in range(ALL_TILES):
        piece = grad_ref[0, :, tile * LANES : (tile + 1) * LANES]
        grad_flat[pl.ds(tile, block, stride=ALL_TILES), :] = piece.astype(jnp.float32)
    grad = grad_flat[...]
    m_new = 0.9 * m_ref[0] + 0.1 * grad
    v_new = 0.99 * v_ref[0] + 0.01 * grad * grad
    m_out[0] = m_new
    v_out[0] = v_new
    step = m_new / (jnp.sqrt(v_new) + 1e-08)
    square = step * step

    @pl.when(pl.program_id(1) == 0)
    def _():
        total_ref[...] = square

    @pl.when(pl.program_id(1) > 0)
    def _():
        total_ref[...] += square

    @pl.when(pl.program_id(1) == pl.num_programs(1) - 1)
    def _():
        by_column = total_ref[0:ALL_TILES, :]
        for row in range(1, block):
            by_column = by_column + total_ref[row * ALL_TILES : (row + 1) * ALL_TILES, :]
        column = lax.broadcasted_iota(jnp.int32, by_column.shape, 0) * LANES
        column = column + lax.broadcasted_iota(jnp.int32, by_column.shape, 1)
        for kind in range(7):
            keep = (column >= STARTS[kind]) & (column < STARTS[kind] + WIDTHS[kind])
            sum_ref[layer, kind] = jnp.sum(jnp.where(keep, by_column, 0.0))


def adam_update(grads, adam_m, adam_v):
    layers, rows, _ = grads.shape
    block = row_block(rows)
    blocks = rows // block
    view = (layers * blocks, block * ALL_TILES, LANES)
    flat_spec = pl.BlockSpec((1,) + view[1:], lambda l, r: (l * blocks + r, 0, 0))
    flat = jax.ShapeDtypeStruct(view, jnp.float32)
    count = layers * rows * HALF
    m_new, v_new, sums = pl.pallas_call(
        adam_kernel,
        out_shape=[flat, flat, jax.ShapeDtypeStruct((layers, 7), jnp.float32)],
        grid_spec=pltpu.PrefetchScalarGridSpec(
            num_scalar_prefetch=0,
            grid=(layers, blocks),
            in_specs=[pl.BlockSpec((1, block, HALF), lambda l, r: (l, r, 0)), flat_spec, flat_spec],
            out_specs=[flat_spec, flat_spec, pl.BlockSpec(memory_space=pltpu.SMEM)],
            scratch_shapes=[pltpu.VMEM(view[1:], jnp.float32), pltpu.VMEM(view[1:], jnp.float32)],
        ),
        cost_estimate=pl.CostEstimate(
            flops=12 * count, bytes_accessed=18 * count, transcendentals=2 * count
        ),
        name="adam_update",
    )(grads, adam_m.reshape(view), adam_v.reshape(view))
    return m_new.reshape(adam_m.shape), v_new.reshape(adam_v.shape), sums


def apply_kernel(wide_ranks, step_ref, core_ref, *refs):
    root_refs = refs[: 2 * GROUP]
    grad_hbm, out_hbm, sum_ref, root_buf, grad_buf, out_buf, root_sem, grad_sem, out_sem = refs[
        2 * GROUP :
    ]
    half = root_refs[0].shape[0]
    core = core_ref[0]

    def columns(rank):
        if rank < wide_ranks:
            return pl.ds(rank * WIDE * LANES, WIDE * LANES)
        return pl.ds((wide_ranks * (WIDE - 1) + rank) * LANES, LANES)

    def root_copy(step, rank, side):
        at = pl.multiple_of((core if side == 0 else 1 - core) * half, half)
        return pltpu.make_async_copy(
            root_refs[2 * step + side],
            root_buf.at[rank, pl.ds(at, half), :],
            root_sem.at[rank, side],
        )

    def grad_copy(rank):
        part = columns(rank)
        return pltpu.make_async_copy(
            grad_hbm.at[:, part], grad_buf.at[:, part], grad_sem.at[rank]
        )

    def out_copy(rank):
        part = columns(rank)
        return pltpu.make_async_copy(out_buf.at[:, part], out_hbm.at[:, part], out_sem.at[rank])

    for rank in range(GROUP):
        grad_copy(rank).start()
        for step in range(GROUP):

            @pl.when(step_ref[rank] == step)
            def _():
                root_copy(step, rank, 0).start()
                root_copy(step, rank, 1).start()

    def run(rank, tile, tiles):
        part = pl.ds(pl.multiple_of(tile * LANES, LANES), tiles * LANES)
        value = jnp.dot(root_buf[rank], grad_buf[:, part], preferred_element_type=jnp.float32)
        value = value.astype(jnp.bfloat16)
        out_buf[:, part] = value
        value = value.astype(jnp.float32)
        sum_ref[rank] = jnp.sum(value * value)

    for rank in range(GROUP):
        grad_copy(rank).wait()
        root_copy(0, rank, 0).wait()
        root_copy(0, rank, 1).wait()
        if rank < wide_ranks:
            run(rank, rank * WIDE, WIDE)
        else:
            run(rank, wide_ranks * (WIDE - 1) + rank, 1)
        out_copy(rank).start()
    for rank in range(GROUP):
        out_copy(rank).wait()


def apply_roots(wide_ranks, steps, core, roots, gathered):
    half, model_rows = roots[0].shape
    cols = gathered.shape[1]
    anywhere = pl.BlockSpec(memory_space=pl.ANY)
    return pl.pallas_call(
        functools.partial(apply_kernel, wide_ranks),
        out_shape=[
            jax.ShapeDtypeStruct((model_rows, cols), jnp.bfloat16),
            jax.ShapeDtypeStruct((GROUP,), jnp.float32),
        ],
        grid_spec=pltpu.PrefetchScalarGridSpec(
            num_scalar_prefetch=2,
            grid=(1,),
            in_specs=[anywhere] * (2 * GROUP + 1),
            out_specs=[anywhere, pl.BlockSpec(memory_space=pltpu.SMEM)],
            scratch_shapes=[
                pltpu.VMEM((GROUP, model_rows, model_rows), jnp.bfloat16),
                pltpu.VMEM((model_rows, cols), jnp.bfloat16),
                pltpu.VMEM((model_rows, cols), jnp.bfloat16),
                pltpu.SemaphoreType.DMA((GROUP, 2)),
                pltpu.SemaphoreType.DMA((GROUP,)),
                pltpu.SemaphoreType.DMA((GROUP,)),
            ],
        ),
        name="apply_roots",
    )(steps, core, *roots, gathered)


def gram_kernel(wide_ranks, step_ref, core_ref, mine_ref, other_ref, *refs):
    out_refs = refs[:GROUP]
    out_buf, out_sem = refs[GROUP:]
    rank = pl.program_id(0)
    half = out_buf.shape[1]
    core = core_ref[0]

    def run(tile, tiles):
        columns = pl.ds(pl.multiple_of(tile * LANES, LANES), tiles * LANES)
        rows = pl.ds(pl.multiple_of(core * half, half), half)
        total = None
        for grad_ref in (mine_ref, other_ref):
            term = lax.dot_general(
                grad_ref[rows, columns],
                grad_ref[:, columns],
                (((1,), (1,)), ((), ())),
                preferred_element_type=jnp.float32,
            )
            total = term if total is None else total + term
        out_buf[rank] = total.astype(jnp.bfloat16)

    @pl.when(rank < wide_ranks)
    def _():
        run(rank * WIDE, WIDE)

    @pl.when(rank >= wide_ranks)
    def _():
        run(wide_ranks * (WIDE - 1) + rank, 1)

    def out_copy(step, at):
        return pltpu.make_async_copy(out_buf.at[at], out_refs[step], out_sem.at[at])

    for step in range(GROUP):

        @pl.when(step_ref[rank] == step)
        def _():
            out_copy(step, rank).start()

    @pl.when(rank == GROUP - 1)
    def _():
        for at in range(GROUP):
            out_copy(0, at).wait()


def part_grams(wide_ranks, steps, core, mine, other):
    model_rows, cols = mine.shape
    half = model_rows // 2
    whole = pl.BlockSpec((model_rows, cols), lambda r, *_: (0, 0))
    return pl.pallas_call(
        functools.partial(gram_kernel, wide_ranks),
        out_shape=[jax.ShapeDtypeStruct((half, model_rows), jnp.bfloat16)] * GROUP,
        grid_spec=pltpu.PrefetchScalarGridSpec(
            num_scalar_prefetch=2,
            grid=(GROUP,),
            in_specs=[whole, whole],
            out_specs=[pl.BlockSpec(memory_space=pl.ANY)] * GROUP,
            scratch_shapes=[
                pltpu.VMEM((GROUP, half, model_rows), jnp.bfloat16),
                pltpu.SemaphoreType.DMA((GROUP,)),
            ],
        ),
        name="part_grams",
    )(steps, core, mine, other)


def update_kernel(
    wide_ranks, base_ref, rank_ref, scale_ref, weight_ref, back_ref, out_ref, done_ref
):
    layer = pl.program_id(0)
    done_ref[0] = layer
    rows = back_ref.shape[1]
    lane = lax.broadcasted_iota(jnp.int32, (rows, LANES), 1)
    for tile in range(ALL_TILES):
        step = None
        for kind in range(7):
            at = tile - TILE0[kind]
            if not 0 <= at < TILES[kind]:
                continue
            matrix = layer * 7 + kind
            rank = rank_ref[matrix]
            if kind >= FIRST_WIDE:
                source, column = at // WIDE, rank * WIDE + at % WIDE
            else:
                source, column = at, rank_tile(rank, wide_ranks)
            piece = back_ref[
                base_ref[matrix] + source, :, pl.ds(pl.multiple_of(column * LANES, LANES), LANES)
            ]
            piece = 0.02 * (scale_ref[matrix] * piece.astype(jnp.float32))
            low = STARTS[kind] - tile * LANES
            step = piece if step is None else jnp.where(lane >= low, piece, step)
        where = pl.ds(tile, rows, stride=ALL_TILES)
        out_ref[0, where, :] = weight_ref[0, where, :] - step


def update_weights(wide_ranks, plan, ratio, weights, returned):
    layers, rows = weights.shape[:2]
    view = (layers, rows * ALL_TILES, LANES)
    flat_spec = pl.BlockSpec((1,) + view[1:], lambda l, *_: (l, 0, 0))
    out, done = pl.pallas_call(
        functools.partial(update_kernel, wide_ranks),
        out_shape=[
            jax.ShapeDtypeStruct(view, jnp.float32),
            jax.ShapeDtypeStruct((1,), jnp.int32),
        ],
        grid_spec=pltpu.PrefetchScalarGridSpec(
            num_scalar_prefetch=3,
            grid=(layers,),
            in_specs=[flat_spec, pl.BlockSpec(returned.shape, lambda l, *_: (0, 0, 0))],
            out_specs=[flat_spec, pl.BlockSpec(memory_space=pltpu.SMEM)],
        ),
        name="update_weights",
    )(plan[3], plan[4], ratio.reshape(-1), weights.reshape(view), returned)
    return out.reshape(weights.shape), done


def swap_cores(value):
    return lax.ppermute(value, "tp", [(0, 1), (1, 0)])


def swap_chips(value, step):
    chips = lax.axis_size("fsdp")
    return lax.ppermute(value, "fsdp", [(i, i ^ step) for i in range(chips)])


def sum_over(value, step):
    return value + sum(swap_chips(value, step * other) for other in range(1, 4))


def refresh(
    wide_ranks, plan, grads, weights, adam_m, adam_v, stats, roots, vec_weight, vec_grad, vec_m, vec_v
):
    chips = lax.axis_size("fsdp")
    chip = lax.axis_index("fsdp")
    core = lax.axis_index("tp").astype(jnp.int32)
    layers = grads.shape[0]
    rows = grads.shape[1]
    model_rows = rows * chips
    cols = slot_tiles(wide_ranks) * LANES
    group_first = chip - chip % GROUP
    kinds = lax.dynamic_slice(plan[1], (group_first,), (GROUP,))
    places = lax.dynamic_slice(plan[2], (group_first,), (GROUP,))
    own_part = (chip % GROUP).astype(jnp.int32)
    owned = jnp.any((places == own_part) & (kinds < NONE))
    core_arg = core.reshape(1)
    steps = places ^ own_part

    outgoing = build_send(wide_ranks, plan, grads[:, :, 0, :])
    arrived = lax.all_to_all(outgoing, "fsdp", split_axis=0, concat_axis=0, tiled=True)
    adam_m_new, adam_v_new, adam_part = adam_update(grads[:, :, 0, :], adam_m, adam_v)
    along_x = swap_chips(roots[0], 1)
    along_y = swap_chips(roots[0], 2)
    along_x, along_y, adam_part = lax.optimization_barrier((along_x, along_y, adam_part))
    forward = jnp.where(core == 0, along_y, along_x)
    across = lax.ppermute(
        forward,
        ("fsdp", "tp"),
        [(2 * i + side, 2 * (i ^ (1 + side)) + side) for i in range(chips) for side in range(2)],
    )
    group_roots = [along_x, along_y, across]
    all_roots = []
    for part in [roots[0]] + group_roots:
        all_roots += [part, swap_cores(part)]

    arrived, all_roots, adam_part = lax.optimization_barrier((arrived, all_roots, adam_part))
    gathered = arrived.reshape(model_rows, cols)
    precond, sums = apply_roots(wide_ranks, steps, core_arg, all_roots, gathered)
    returned = lax.all_to_all(
        precond.reshape(chips, rows, cols), "fsdp", split_axis=0, concat_axis=0, tiled=True
    )
    ranks = jnp.arange(GROUP, dtype=jnp.int32)
    is_here = (plan[3] == group_first)[:, None] & (plan[4][:, None] == ranks[None, :])
    shampoo_part = jnp.sum(jnp.where(is_here, sums[None, :], 0.0), axis=1).reshape(layers, 7)
    totals = jnp.stack([adam_part, shampoo_part])
    totals = totals + swap_cores(totals)
    beside = [totals] + [swap_chips(totals, step) for step in range(1, GROUP)]
    grams = part_grams(wide_ranks, steps, core_arg, gathered, swap_cores(gathered))
    grams, beside = lax.optimization_barrier((grams, beside))
    totals = sum(beside)
    step = GROUP
    while step < chips:
        totals = sum_over(totals, step)
        step = 4 * step
    ratio = jnp.sqrt(totals[0]) / (jnp.sqrt(totals[1]) + 1e-06)
    terms = [grams[0]] + [swap_chips(grams[step], step) for step in range(1, GROUP)]

    weights_new, done = update_weights(wide_ranks, plan, ratio, weights, returned)

    stat_term = sum(term.astype(jnp.float32) for term in terms)
    owned = owned & (done[0] >= 0)
    stats_new = jnp.where(owned, 0.9 * stats[0] + 0.1 * stat_term, stats[0])[None]

    vec_float = vec_grad.astype(jnp.float32)
    vec_m_new = 0.9 * vec_m + 0.1 * vec_float
    vec_v_new = 0.99 * vec_v + 0.01 * vec_float * vec_float
    vec_weight_new = vec_weight - 0.02 * vec_m_new / (jnp.sqrt(vec_v_new) + 1e-08)
    return (weights_new, adam_m_new, adam_v_new, stats_new, vec_weight_new, vec_m_new, vec_v_new)


def on_device(owner, *arrays):
    plan = make_plan(owner, lax.axis_size("fsdp"))
    branches = [functools.partial(refresh, wide_ranks) for wide_ranks in range(2, GROUP + 1)]
    return lax.switch(plan[5][0] - 2, branches, plan, *arrays)


def solution(mesh):
    matrix = P(None, "fsdp", "tp", None)
    slot = P("fsdp", "tp", None)
    vector = P(None, ("fsdp", "tp"))
    return jax.shard_map(
        on_device,
        mesh=mesh,
        in_specs=(P(), matrix, matrix, matrix, matrix, slot, slot, vector, vector, vector, vector),
        out_specs=(matrix, matrix, matrix, slot, vector, vector, vector),
        check_vma=False,
    )
```

time: 253 us -> 214 us (0.85)
  blocking collectives: 72.1 us -> 0 us
  starting transfers between devices: 21 us -> 59.9 us
  local copies, waits for them, and re-layouts: 18 us -> 1.87 us
  other arithmetic: 16.7 us -> 3.64 us
  Pallas kernels: 34.8 us -> 47.3 us
  waiting for transfers between devices: 88.5 us -> 96 us
    all_to_all x1 -> x0, blocking collectives: 72.1 us -> none  [refresh(): lax.all_to_all(outgoing, 'fsdp', split_axis=0, concat_axis=0, tiled=True)]
    all_to_all x1, waiting for transfers between devices: 27.2 us -> 0.01 us  [refresh(): lax.all_to_all(outgoing, 'fsdp', split_axis=0, concat_axis=0, tiled=True)]
    ppermute x7 -> x11, starting transfers between devices: 11.7 us -> 36.1 us  [swap_chips(): return lax.ppermute(value, 'fsdp', [(i, i ^ step) for i in range(chips)])]
    ppermute x0 -> x1, waiting for transfers between devices: none -> 19 us  [refresh(): lax.ppermute(forward, ('fsdp', 'tp'), [(2 * i + side, 2 * (i ^ 1 + side)...]
    cond x26, local copies, waits for them, and re-layouts: 15.4 us -> 0.06 us  [the longest x2 13.6 us: on_device(): return lax.switch(plan[5][0] - 2, branches, plan, *arrays)]
    pallas_call x2 -> x3, Pallas kernels: 14.1 us -> 28.4 us  [the longest x1 12.5 us: adam_update(): pl.pallas_call(adam_kernel, out_shape=[flat, flat, jax.ShapeDtypeStruct((...]
    ppermute x7 -> x11, waiting for transfers between devices: 60.1 us -> 70 us  [swap_chips(): return lax.ppermute(value, 'fsdp', [(i, i ^ step) for i in range(chips)])]
    all_to_all x1, starting transfers between devices: 4.64 us -> 11.6 us  [refresh(): lax.all_to_all(precond.reshape(chips, rows, cols), 'fsdp', split_axis=0,...]
  transfers between devices with their start and end apart: 12 -> 20, of which waited for: 8 -> 6; matrix products, arithmetic and copies ran while one was open for 13% -> 1% of each run, Pallas kernels for 8% -> 13%
where the time goes in v3:
time: 214 us; the launch traced here: 212 us
  waiting for transfers between devices  96 us (45%)
  starting transfers between devices  59.9 us (28%)
  Pallas kernels  47.3 us (22%)
  other arithmetic  3.64 us (2%)
    ppermute x11, waiting for transfers between devices, swap_chips(): return lax.ppermute(value, 'fsdp', [(i, i ^ step) for i in range(chips)])  70 us
    ppermute x11, starting transfers between devices, swap_chips(): return lax.ppermute(value, 'fsdp', [(i, i ^ step) for i in range(chips)])  36.1 us
    ppermute x1, waiting for transfers between devices, refresh(): lax.ppermute(forward, ('fsdp', 'tp'), [(2 * i + side, 2 * (i ^ 1 + side)...  19 us
    pallas_call x1, Pallas kernels, adam_update(): pl.pallas_call(adam_kernel, out_shape=[flat, flat, jax.ShapeDtypeStruct((...  12.5 us
    all_to_all x1, starting transfers between devices, refresh(): lax.all_to_all(precond.reshape(chips, rows, cols), 'fsdp', split_axis=0,...  11.6 us
    pallas_call x1, Pallas kernels, apply_roots(): pl.pallas_call(functools.partial(apply_kernel, wide_ranks), out_shape=[ja...  11.5 us
    pallas_call x1, Pallas kernels, part_grams(): pl.pallas_call(functools.partial(gram_kernel, wide_ranks), out_shape=[jax...  10.2 us
    all_to_all x1, starting transfers between devices, refresh(): lax.all_to_all(outgoing, 'fsdp', split_axis=0, concat_axis=0, tiled=True)  8.62 us
  transfers between devices with their start and end apart: 20, of which 6 were waited for; matrix products, arithmetic and copies ran while one was open for 1% of the time, Pallas kernels for 13%

profile of v3, /device:TPU:0, one launch (start us, length us, event | category | flops | bytes accessed | tf_op | source)
XLA Modules:
  0.0 212.1 jit_solution(4312257139245444606)
XLA Ops:
  0.6 1.9 plan.1
  3.2 207.7 %conditional.1 = (f32[1,448,896]{2,1,0:T(8,128)S(1)}, f32[2,92]{1,0:T(2,128)S(1)}, f32[2,92]{1,0:T(2,128)S(1)}, f32[2,92]{1,0:T(2,128)S(1)}, f32[2,56,1,8320]{3,...) conditional(s32[]{:T(128)} %bitcast.48, (s32[16]{0:T(128)S(1)}, ...), branch_computations={%region_0.3_spmd, %region_3.6_spmd, %region_6.9_spmd} | conditional | flops 16001730 | bytes 133547808 | solution.py:523
  3.3 5.5 %build_send.4 = bf16[16,56,2048]{2,1,0:T(8,128)(2,1)} custom-call(s32[16]{0:T(128)S(1)} %get-tuple-element.140.layer_ref, s32[16]{0:T(128)S(1)} %get-tuple-element.141.kind_ref, bf16[2,56,8320]{2,1,0:T(8,128)(2,1)} %bitcast.78), custom_call_target="tpu_custom_call" | custom-call | tf_op jit(solution)/shard_map/cond/branch_1_fun/build_send/pallas_call | solution.py:160
  8.7 8.6 %all-to-all-start.2 = ((bf16[16,56,2048]{2,1,0:T(8,128)(2,1)}), bf16[16,56,2048]{2,1,0:T(8,128)(2,1)}, u32[]{:S(2)}, u32[]{:S(2)}) async-start(bf16[16,56,2048]{2,1,0:T(8,128)(2,1)} %build_send.4), calls=%async_computation.2 | async-start | bytes 7340032 | tf_op jit(solution)/shard_map/cond/branch_1_fun/all_to_all | solution.py:469
  17.4 1.9 collective-permute-start.20
  19.3 1.5 collective-permute-start.19
  20.8 12.5 %adam_update.4 = (f32[14,520,128]{2,1,0:T(8,128)}, f32[14,520,128]{2,1,0:T(8,128)}, f32[2,7]{1,0:T(2,128)}) custom-call(bf16[2,56,8320]{2,1,0:T(8,128)(2,1)S(1)} %bitcast.79, f32[14,520,128]{2,1,0:T(8,128)} %bitcast.83, f32[14,520,128]{2,1,0:T(8,128)} %bitcast.86), custom_call_target="tpu_custom_call" | custom-call | flops 11182080 | bytes 16773120 | tf_op jit(solution)/shard_map/cond/branch_1_fun/adam_update/pallas_call | solution.py:215
  33.2 35.9 %collective-permute-done.20.refs_4_ = bf16[448,896]{1,0:T(8,128)(2,1)S(1)} collective-permute-done((bf16[448,896]{1,0:T(8,128)(2,1)S(1)}, bf16[448,896]{1,0:T(8,128)(2,1)S(1)}, u32[]{:S(2)}, u32[]{:S(2)}) %collective-permute-start.20) | collective-permute-done | bytes 802848 | tf_op jit(solution)/shard_map/cond/branch_1_fun/ppermute | solution.py:443
  69.3 2.5 %collective-permute-start.23 = (bf16[448,896]{1,0:T(8,128)(2,1)S(1)}, bf16[448,896]{1,0:T(8,128)(2,1)S(1)}, u32[]{:S(2)}, u32[]{:S(2)}) collective-permute-start(bf16[448,896]{1,0:T(8,128)(2,1)S(1)} %broadcast_select_fusion.1), channel_id=1, source_target_pairs={{0,2},{1,5},{2,0},{3,7},{4,6},{5,1},{6,4},{7,3},{8,10},{9,13},{10,... | collective-permute-start | bytes 2408456 | tf_op jit(solution)/shard_map/cond/branch_1_fun/ppermute | solution.py:475
  71.8 0.5 collective-permute-start.21
  72.3 19.0 %collective-permute-done.23.refs_6_ = bf16[448,896]{1,0:T(8,128)(2,1)S(1)} collective-permute-done((bf16[448,896]{1,0:T(8,128)(2,1)S(1)}, bf16[448,896]{1,0:T(8,128)(2,1)S(1)}, u32[]{:S(2)}, u32[]{:S(2)}) %collective-permute-start.23) | collective-permute-done | bytes 802848 | tf_op jit(solution)/shard_map/cond/branch_1_fun/ppermute | solution.py:475
  91.3 0.7 broadcast_xor_fusion.1.step_ref
  92.0 1.7 collective-permute-done.24.refs_7_
  93.8 11.5 %apply_roots.4 = (bf16[896,2048]{1,0:T(8,128)(2,1)}, f32[4]{0:T(128)}) custom-call(s32[4]{0:T(128)} %broadcast_xor_fusion.1.step_ref, s32[1]{0:T(128)} %bitcast.16.core_ref, bf16[448,896]{1,0:T(8,128)(2,1)S(1)} %bitcast.98, bf16[448,896]{1,0:T(8,128)(2,1)} %copy-done.22, bf16[448,896]{1,0:T(8,128)(2,1)} %collective-permute-done.19.refs_2_, ...), custom_call_target="tpu_custom_call" | custom-call | tf_op jit(solution)/shard_map/cond/branch_1_fun/apply_roots/pallas_call | solution.py:298
  105.3 11.6 %all-to-all-start.3 = ((bf16[16,56,2048]{2,1,0:T(8,128)(2,1)}), bf16[16,56,2048]{2,1,0:T(8,128)(2,1)}, u32[]{:S(2)}, u32[]{:S(2)}) async-start(bf16[16,56,2048]{2,1,0:T(8,128)(2,1)} %bitcast.104), calls=%async_computation.3 | async-start | bytes 7340032 | tf_op jit(solution)/shard_map/cond/branch_1_fun/all_to_all | solution.py:488
  117.2 0.5 collective-permute-start.26
  117.7 5.3 %collective-permute-done.26 = f32[2,2,7]{2,1,0:T(2,128)S(1)} collective-permute-done((f32[2,2,7]{2,1,0:T(2,128)S(1)}, f32[2,2,7]{2,1,0:T(2,128)S(1)}, u32[]{:S(2)}, u32[]{:S(2)}) %collective-permute-start.26) | collective-permute-done | bytes 144 | tf_op jit(solution)/shard_map/cond/branch_1_fun/ppermute | solution.py:438
  123.0 2.8 %collective-permute-start.29 = (f32[2,2,7]{2,1,0:T(2,128)S(1)}, f32[2,2,7]{2,1,0:T(2,128)S(1)}, u32[]{:S(2)}, u32[]{:S(2)}) collective-permute-start(f32[2,2,7]{2,1,0:T(2,128)S(1)} %fusion.15), channel_id=1, source_target_pairs={{0,6},{2,4},{4,2},{6,0},{8,14},{10,12},{12,10},{14,8},{16,22},{18,... | collective-permute-start | bytes 344 | tf_op jit(solution)/shard_map/cond/branch_1_fun/ppermute | solution.py:443
  125.8 0.6 collective-permute-start.28
  126.6 10.2 %part_grams.4 = (bf16[448,896]{1,0:T(8,128)(2,1)}, bf16[448,896]{1,0:T(8,128)(2,1)}, bf16[448,896]{1,0:T(8,128)(2,1)}, bf16[448,896]{1,0:T(8,128)(2,1)}) custom-call(s32[4]{0:T(128)} %broadcast_xor_fusion.1.step_ref, s32[1]{0:T(128)} %bitcast.16.core_ref, bf16[896,2048]{1,0:T(8,128)(2,1)} %bitcast.22.mine_ref.refs_8_, ...), custom_call_target="tpu_custom_call" | custom-call | tf_op jit(solution)/shard_map/cond/branch_1_fun/part_grams/pallas_call | solution.py:370
  136.9 1.8 collective-permute-start.33
  138.7 1.5 collective-permute-start.34
  140.2 0.2 collective-permute-start.35
  140.4 5.7 %collective-permute-start.32 = (f32[2,2,7]{2,1,0:T(2,128)S(1)}, f32[2,2,7]{2,1,0:T(2,128)S(1)}, u32[]{:S(2)}, u32[]{:S(2)}) collective-permute-start(f32[2,2,7]{2,1,0:T(2,128)S(1)} %add_add_fusion.3), channel_id=1, source_target_pairs={{0,24},{2,26},{4,28},{6,30},{8,16},{10,18},{12,20},{14,22},{16,8},... | collective-permute-start | bytes 344 | tf_op jit(solution)/shard_map/cond/branch_1_fun/ppermute | solution.py:443
  146.2 33.2 %collective-permute-done.32 = f32[2,2,7]{2,1,0:T(2,128)S(1)} collective-permute-done((f32[2,2,7]{2,1,0:T(2,128)S(1)}, f32[2,2,7]{2,1,0:T(2,128)S(1)}, u32[]{:S(2)}, u32[]{:S(2)}) %collective-permute-start.32) | collective-permute-done | bytes 144 | tf_op jit(solution)/shard_map/cond/branch_1_fun/ppermute | solution.py:443
  179.4 19.8 %collective-permute-start.30 = (f32[2,2,7]{2,1,0:T(2,128)S(1)}, f32[2,2,7]{2,1,0:T(2,128)S(1)}, u32[]{:S(2)}, u32[]{:S(2)}) collective-permute-start(f32[2,2,7]{2,1,0:T(2,128)S(1)} %add_add_fusion.3), channel_id=1, source_target_pairs={{0,8},{2,10},{4,12},{6,14},{8,0},{10,2},{12,4},{14,6},{16,24},{18,... | collective-permute-start | bytes 344 | tf_op jit(solution)/shard_map/cond/branch_1_fun/ppermute | solution.py:443
  199.2 0.7 and_reduce_fusion.1
  199.9 0.9 collective-permute-done.30
  200.8 0.6 div.25.scale_ref
  201.4 5.7 %update_weights.4 = (f32[2,3640,128]{2,1,0:T(8,128)}, s32[1]{0:T(128)}) custom-call(s32[14]{0:T(128)S(1)} %get-tuple-element.137.base_ref, s32[14]{0:T(128)S(1)} %get-tuple-element.138.rank_ref, f32[14]{0:T(128)} %div.25.scale_ref, f32[2,3640,128]{2,1,0:T(8,128)} %bitcast.89, bf16[16,56,2048]{2,1,0:T(8,128)(2,1)} %all-to-all-done.3.back_ref), custom_call_target="tpu_custom_call" | custom-call | tf_op jit(solution)/shard_map/cond/branch_1_fun/update_weights/pallas_call | solution.py:420
  208.5 2.0 fusion.9
  211.0 1.1 copy-done.13
  (63 shorter events, 0.8 us)
Async XLA Ops:
  8.7 8.6 %copy-start.8 = (bf16[1,448,896]{2,1,0:T(8,128)(2,1)S(1)}, bf16[1,448,896]{2,1,0:T(8,128)(2,1)}, u32[]{:S(2)}) copy-start(bf16[1,448,896]{2,1,0:T(8,128)(2,1)} %get-tuple-element.143) | copy-start | bytes 2408452 | tf_op jit(solution)/shard_map/cond
  8.7 12.0 %copy-start.1 = (bf16[2,56,1,8320]{3,1,2,0:T(8,128)(2,1)S(1)}, bf16[2,56,1,8320]{3,1,2,0:T(8,128)(2,1)}, u32[]{:S(2)}) copy-start(bf16[2,56,1,8320]{3,1,2,0:T(8,128)(2,1)} %get-tuple-element.325) | copy-start | bytes 5591044 | tf_op jit(solution)/shard_map/cond
  8.7 85.0 %all-to-all-start.2 = ((bf16[16,56,2048]{2,1,0:T(8,128)(2,1)}), bf16[16,56,2048]{2,1,0:T(8,128)(2,1)}, u32[]{:S(2)}, u32[]{:S(2)}) async-start(bf16[16,56,2048]{2,1,0:T(8,128)(2,1)} %build_send.4), calls=%async_computation.2 | async-start | bytes 7340032 | tf_op jit(solution)/shard_map/cond/branch_1_fun/all_to_all | solution.py:469
  17.4 51.8 %collective-permute-start.20 = (bf16[448,896]{1,0:T(8,128)(2,1)S(1)}, bf16[448,896]{1,0:T(8,128)(2,1)S(1)}, u32[]{:S(2)}, u32[]{:S(2)}) collective-permute-start(bf16[448,896]{1,0:T(8,128)(2,1)S(1)} %bitcast.95), channel_id=1, source_target_pairs={{0,4},{2,6},{4,0},{6,2},{8,12},{10,14},{12,8},{14,10},{16,20},{18,... | collective-permute-start | bytes 2408456 | tf_op jit(solution)/shard_map/cond/branch_1_fun/ppermute | solution.py:443
  19.3 49.8 %collective-permute-start.19 = (bf16[448,896]{1,0:T(8,128)(2,1)S(1)}, bf16[448,896]{1,0:T(8,128)(2,1)}, u32[]{:S(2)}, u32[]{:S(2)}) collective-permute-start(bf16[448,896]{1,0:T(8,128)(2,1)S(1)} %bitcast.96), channel_id=1, source_target_pairs={{0,2},{2,0},{4,6},{6,4},{8,10},{10,8},{12,14},{14,12},{16,18},{18,... | collective-permute-start | bytes 2408456 | tf_op jit(solution)/shard_map/cond/branch_1_fun/ppermute | solution.py:443
  69.2 24.6 %copy-start.12 = (bf16[448,896]{1,0:T(8,128)(2,1)}, bf16[448,896]{1,0:T(8,128)(2,1)S(1)}, u32[]{:S(2)}) copy-start(bf16[448,896]{1,0:T(8,128)(2,1)S(1)} %collective-permute-done.20.refs_4_) | copy-start | bytes 2408452 | tf_op jit(solution)/shard_map/cond
  69.3 22.0 %collective-permute-start.23 = (bf16[448,896]{1,0:T(8,128)(2,1)S(1)}, bf16[448,896]{1,0:T(8,128)(2,1)S(1)}, u32[]{:S(2)}, u32[]{:S(2)}) collective-permute-start(bf16[448,896]{1,0:T(8,128)(2,1)S(1)} %broadcast_select_fusion.1), channel_id=1, source_target_pairs={{0,2},{1,5},{2,0},{3,7},{4,6},{5,1},{6,4},{7,3},{8,10},{9,13},{10,... | collective-permute-start | bytes 2408456 | tf_op jit(solution)/shard_map/cond/branch_1_fun/ppermute | solution.py:475
  71.8 20.2 %collective-permute-start.18 = (bf16[448,896]{1,0:T(8,128)(2,1)S(1)}, bf16[448,896]{1,0:T(8,128)(2,1)S(1)}, u32[]{:S(2)}, u32[]{:S(2)}) collective-permute-start(bf16[448,896]{1,0:T(8,128)(2,1)S(1)} %bitcast.97), channel_id=1, source_target_pairs={{0,1},{1,0},{2,3},{3,2},{4,5},{5,4},{6,7},{7,6},{8,9},{9,8},{10,11... | collective-permute-start | bytes 2408456 | tf_op jit(solution)/shard_map/cond/branch_1_fun/ppermute | solution.py:438
  71.8 20.2 %collective-permute-start.21 = (bf16[448,896]{1,0:T(8,128)(2,1)}, bf16[448,896]{1,0:T(8,128)(2,1)}, u32[]{:S(2)}, u32[]{:S(2)}) collective-permute-start(bf16[448,896]{1,0:T(8,128)(2,1)} %collective-permute-done.19.refs_2_), channel_id=1, source_target_pairs={{0,1},{1,0},{2,3},{3,2},{4,5},{5,4},{6,7},{7,6},{8,9},{9,8},{10,11... | collective-permute-start | bytes 2408456 | tf_op jit(solution)/shard_map/cond/branch_1_fun/ppermute | solution.py:438
  72.3 19.7 %collective-permute-start.22 = (bf16[448,896]{1,0:T(8,128)(2,1)S(1)}, bf16[448,896]{1,0:T(8,128)(2,1)}, u32[]{:S(2)}, u32[]{:S(2)}) collective-permute-start(bf16[448,896]{1,0:T(8,128)(2,1)S(1)} %collective-permute-done.20.refs_4_), channel_id=1, source_target_pairs={{0,1},{1,0},{2,3},{3,2},{4,5},{5,4},{6,7},{7,6},{8,9},{9,8},{10,11... | collective-permute-start | bytes 2408456 | tf_op jit(solution)/shard_map/cond/branch_1_fun/ppermute | solution.py:438
  91.3 2.5 %copy-start.21 = (bf16[448,896]{1,0:T(8,128)(2,1)}, bf16[448,896]{1,0:T(8,128)(2,1)S(1)}, u32[]{:S(2)}) copy-start(bf16[448,896]{1,0:T(8,128)(2,1)S(1)} %collective-permute-done.23.refs_6_) | copy-start | bytes 2408452 | tf_op jit(solution)/shard_map/cond
  91.3 2.4 %collective-permute-start.24 = (bf16[448,896]{1,0:T(8,128)(2,1)S(1)}, bf16[448,896]{1,0:T(8,128)(2,1)}, u32[]{:S(2)}, u32[]{:S(2)}) collective-permute-start(bf16[448,896]{1,0:T(8,128)(2,1)S(1)} %collective-permute-done.23.refs_6_), channel_id=1, source_target_pairs={{0,1},{1,0},{2,3},{3,2},{4,5},{5,4},{6,7},{7,6},{8,9},{9,8},{10,11... | collective-permute-start | bytes 2408456 | tf_op jit(solution)/shard_map/cond/branch_1_fun/ppermute | solution.py:438
  105.3 11.7 %copy-start.42 = (f32[4]{0:T(128)S(1)}, f32[4]{0:T(128)}, u32[]{:S(2)}) copy-start(f32[4]{0:T(128)} %get-tuple-element.164) | copy-start | bytes 52 | tf_op jit(solution)/shard_map/cond
  105.3 11.9 %copy-start.36 = (f32[2,7]{1,0:T(2,128)S(1)}, f32[2,7]{1,0:T(2,128)}, u32[]{:S(2)}) copy-start(f32[2,7]{1,0:T(2,128)} %get-tuple-element.155) | copy-start | bytes 172 | tf_op jit(solution)/shard_map/cond
  105.3 96.1 %all-to-all-start.3 = ((bf16[16,56,2048]{2,1,0:T(8,128)(2,1)}), bf16[16,56,2048]{2,1,0:T(8,128)(2,1)}, u32[]{:S(2)}, u32[]{:S(2)}) async-start(bf16[16,56,2048]{2,1,0:T(8,128)(2,1)} %bitcast.104), calls=%async_computation.3 | async-start | bytes 7340032 | tf_op jit(solution)/shard_map/cond/branch_1_fun/all_to_all | solution.py:488
  116.9 9.7 %collective-permute-start.25 = (bf16[896,2048]{1,0:T(8,128)(2,1)}, bf16[896,2048]{1,0:T(8,128)(2,1)}, u32[]{:S(2)}, u32[]{:S(2)}) collective-permute-start(bf16[896,2048]{1,0:T(8,128)(2,1)} %bitcast.22.mine_ref.refs_8_), channel_id=1, source_target_pairs={{0,1},{1,0},{2,3},{3,2},{4,5},{5,4},{6,7},{7,6},{8,9},{9,8},{10,11... | collective-permute-start | bytes 11010056 | tf_op jit(solution)/shard_map/cond/branch_1_fun/ppermute | solution.py:438
  117.2 5.8 %collective-permute-start.26 = (f32[2,2,7]{2,1,0:T(2,128)S(1)}, f32[2,2,7]{2,1,0:T(2,128)S(1)}, u32[]{:S(2)}, u32[]{:S(2)}) collective-permute-start(f32[2,2,7]{2,1,0:T(2,128)S(1)} %pad_maximum_fusion.1), channel_id=1, source_target_pairs={{0,1},{1,0},{2,3},{3,2},{4,5},{5,4},{6,7},{7,6},{8,9},{9,8},{10,11... | collective-permute-start | bytes 344 | tf_op jit(solution)/shard_map/cond/branch_1_fun/ppermute | solution.py:438
  123.0 23.1 %copy-start.24 = (f32[2,92]{1,0:T(2,128)S(1)}, f32[2,92]{1,0:T(2,128)}, u32[]{:S(2)}) copy-start(f32[2,92]{1,0:T(2,128)} %get-tuple-element.181) | copy-start | bytes 2212 | tf_op jit(solution)/shard_map/cond
  123.0 23.1 %copy-start.27 = (f32[2,92]{1,0:T(2,128)S(1)}, f32[2,92]{1,0:T(2,128)}, u32[]{:S(2)}) copy-start(f32[2,92]{1,0:T(2,128)} %get-tuple-element.183) | copy-start | bytes 2212 | tf_op jit(solution)/shard_map/cond
  123.0 23.1 %copy-start.30 = (f32[2,92]{1,0:T(2,128)S(1)}, f32[2,92]{1,0:T(2,128)}, u32[]{:S(2)}) copy-start(f32[2,92]{1,0:T(2,128)} %get-tuple-element.180) | copy-start | bytes 2212 | tf_op jit(solution)/shard_map/cond
  123.0 23.1 %copy-start.33 = (bf16[2,92]{1,0:T(2,128)(2,1)S(1)}, bf16[2,92]{1,0:T(2,128)(2,1)}, u32[]{:S(2)}) copy-start(bf16[2,92]{1,0:T(2,128)(2,1)} %get-tuple-element.182) | copy-start | bytes 1108 | tf_op jit(solution)/shard_map/cond
  123.0 13.8 %collective-permute-start.29 = (f32[2,2,7]{2,1,0:T(2,128)S(1)}, f32[2,2,7]{2,1,0:T(2,128)S(1)}, u32[]{:S(2)}, u32[]{:S(2)}) collective-permute-start(f32[2,2,7]{2,1,0:T(2,128)S(1)} %fusion.15), channel_id=1, source_target_pairs={{0,6},{2,4},{4,2},{6,0},{8,14},{10,12},{12,10},{14,8},{16,22},{18,... | collective-permute-start | bytes 344 | tf_op jit(solution)/shard_map/cond/branch_1_fun/ppermute | solution.py:443
  125.8 11.0 %collective-permute-start.28 = (f32[2,2,7]{2,1,0:T(2,128)S(1)}, f32[2,2,7]{2,1,0:T(2,128)S(1)}, u32[]{:S(2)}, u32[]{:S(2)}) collective-permute-start(f32[2,2,7]{2,1,0:T(2,128)S(1)} %fusion.15), channel_id=1, source_target_pairs={{0,4},{2,6},{4,0},{6,2},{8,12},{10,14},{12,8},{14,10},{16,20},{18,... | collective-permute-start | bytes 344 | tf_op jit(solution)/shard_map/cond/branch_1_fun/ppermute | solution.py:443
  126.4 10.4 %collective-permute-start.27 = (f32[2,2,7]{2,1,0:T(2,128)S(1)}, f32[2,2,7]{2,1,0:T(2,128)S(1)}, u32[]{:S(2)}, u32[]{:S(2)}) collective-permute-start(f32[2,2,7]{2,1,0:T(2,128)S(1)} %fusion.15), channel_id=1, source_target_pairs={{0,2},{2,0},{4,6},{6,4},{8,10},{10,8},{12,14},{14,12},{16,18},{18,... | collective-permute-start | bytes 344 | tf_op jit(solution)/shard_map/cond/branch_1_fun/ppermute | solution.py:443
  136.9 71.6 %collective-permute-start.33 = (bf16[448,896]{1,0:T(8,128)(2,1)}, bf16[448,896]{1,0:T(8,128)(2,1)S(1)}, u32[]{:S(2)}, u32[]{:S(2)}) collective-permute-start(bf16[448,896]{1,0:T(8,128)(2,1)} %get-tuple-element.177), channel_id=1, source_target_pairs={{0,2},{2,0},{4,6},{6,4},{8,10},{10,8},{12,14},{14,12},{16,18},{18,... | collective-permute-start | bytes 2408456 | tf_op jit(solution)/shard_map/cond/branch_1_fun/ppermute | solution.py:443
  138.7 69.7 %collective-permute-start.34 = (bf16[448,896]{1,0:T(8,128)(2,1)}, bf16[448,896]{1,0:T(8,128)(2,1)}, u32[]{:S(2)}, u32[]{:S(2)}) collective-permute-start(bf16[448,896]{1,0:T(8,128)(2,1)} %get-tuple-element.178), channel_id=1, source_target_pairs={{0,4},{2,6},{4,0},{6,2},{8,12},{10,14},{12,8},{14,10},{16,20},{18,... | collective-permute-start | bytes 2408456 | tf_op jit(solution)/shard_map/cond/branch_1_fun/ppermute | solution.py:443
  140.2 68.3 %collective-permute-start.35 = (bf16[448,896]{1,0:T(8,128)(2,1)}, bf16[448,896]{1,0:T(8,128)(2,1)}, u32[]{:S(2)}, u32[]{:S(2)}) collective-permute-start(bf16[448,896]{1,0:T(8,128)(2,1)} %get-tuple-element.179), channel_id=1, source_target_pairs={{0,6},{2,4},{4,2},{6,0},{8,14},{10,12},{12,10},{14,8},{16,22},{18,... | collective-permute-start | bytes 2408456 | tf_op jit(solution)/shard_map/cond/branch_1_fun/ppermute | solution.py:443
  140.4 39.0 %collective-permute-start.32 = (f32[2,2,7]{2,1,0:T(2,128)S(1)}, f32[2,2,7]{2,1,0:T(2,128)S(1)}, u32[]{:S(2)}, u32[]{:S(2)}) collective-permute-start(f32[2,2,7]{2,1,0:T(2,128)S(1)} %add_add_fusion.3), channel_id=1, source_target_pairs={{0,24},{2,26},{4,28},{6,30},{8,16},{10,18},{12,20},{14,22},{16,8},... | collective-permute-start | bytes 344 | tf_op jit(solution)/shard_map/cond/branch_1_fun/ppermute | solution.py:443
  146.1 53.7 %collective-permute-start.31 = (f32[2,2,7]{2,1,0:T(2,128)S(1)}, f32[2,2,7]{2,1,0:T(2,128)S(1)}, u32[]{:S(2)}, u32[]{:S(2)}) collective-permute-start(f32[2,2,7]{2,1,0:T(2,128)S(1)} %add_add_fusion.3), channel_id=1, source_target_pairs={{0,16},{2,18},{4,20},{6,22},{8,24},{10,26},{12,28},{14,30},{16,0},... | collective-permute-start | bytes 344 | tf_op jit(solution)/shard_map/cond/branch_1_fun/ppermute | solution.py:443
  179.4 21.3 %collective-permute-start.30 = (f32[2,2,7]{2,1,0:T(2,128)S(1)}, f32[2,2,7]{2,1,0:T(2,128)S(1)}, u32[]{:S(2)}, u32[]{:S(2)}) collective-permute-start(f32[2,2,7]{2,1,0:T(2,128)S(1)} %add_add_fusion.3), channel_id=1, source_target_pairs={{0,8},{2,10},{4,12},{6,14},{8,0},{10,2},{12,4},{14,6},{16,24},{18,... | collective-permute-start | bytes 344 | tf_op jit(solution)/shard_map/cond/branch_1_fun/ppermute | solution.py:443
  201.4 7.1 %copy-start.4 = (f32[1,448,896]{2,1,0:T(8,128)S(1)}, f32[1,448,896]{2,1,0:T(8,128)}, u32[]{:S(2)}) copy-start(f32[1,448,896]{2,1,0:T(8,128)} %get-tuple-element.175) | copy-start | bytes 4816900 | tf_op jit(solution)/shard_map/cond
  201.4 7.1 %copy-start.15 = (bf16[448,896]{1,0:T(8,128)(2,1)S(1)}, bf16[448,896]{1,0:T(8,128)(2,1)}, u32[]{:S(2)}) copy-start(bf16[448,896]{1,0:T(8,128)(2,1)} %get-tuple-element.176) | copy-start | bytes 2408452 | tf_op jit(solution)/shard_map/cond
  (5 other events, 6.3 us)
